TPU v7x, 512 devices: a whole 4x4x16 slice. The times are simulated.
512 devices in a mesh: dp: 32 (over x, z_lo), label: 16 (over y, z_hi, core).
Axes of the slice: x: 4, y: 4, z: 16 (z_hi: 2, z_lo: 8; z = z_hi * 8 + z_lo), core: 2. Of those that a mesh axis runs over, the one named last changes fastest.
Arguments:
- queries: bfloat16 [16384, 1024], P('dp', 'label'), may hold values from -6 to 6
- positives: int32 [16384, 8], P('dp'), may hold values from 0 to 16383, all different within a row
- counts: int32 [16384], P('dp'), may hold values from 1 to 8
- weight: bfloat16 [16384, 1024], P('label'), may hold values from -0.1875 to 0.1875
- master: float32 [16384, 1024], P(('label', 'dp')), may hold values from -0.1875 to 0.1875
- moment_one: float32 [16384, 1024], P(('label', 'dp')), may hold values from -0.024 to 0.024
- moment_two: float32 [16384, 1024], P(('label', 'dp')), may hold values from 1e-08 to 1e-06
Outputs:
- new_weight: bfloat16 [16384, 1024], P('label')
- new_master: float32 [16384, 1024], P(('label', 'dp'))
- new_one: float32 [16384, 1024], P(('label', 'dp'))
- new_two: float32 [16384, 1024], P(('label', 'dp'))
Inputs may be any that keep to these rules, and one draw needn't show every extreme that they name: `positives`: the ids in one row are distinct, and every label id appears in some row.
All inputs are finite; a program needn't handle non-finite values.
Results may differ from a plain program's by a relative error of at most 0.0031.
Values may be sent and summed in bfloat16 or wider, within the bound.
No kernel may reach another device: no remote copies, remote signals or barrier semaphores. Data moves between devices by JAX's collectives and lax.ppermute only.
A program may use at most 64 MiB of HBM per device.

v0:
```python
import jax
import jax.numpy as jnp
from jax import lax
from jax.sharding import Mesh
from jax.sharding import PartitionSpec as P

ADAM_STEP = 10
DP = ("dp_0", "dp_1")
LABEL_DP = ("label", "dp_0", "dp_1")


def joined_along(tiles, dim):
    tiles = jnp.moveaxis(tiles, 0, dim)
    lengths = tiles.shape
    return tiles.reshape(*lengths[:dim], lengths[dim] * lengths[dim + 1], *lengths[dim + 2 :])


def sent_to_all(array, axis):
    count = lax.axis_size(axis)
    return lax.all_to_all(
        jnp.broadcast_to(array[None], (count, *array.shape)), axis, 0, 0, tiled=True
    )


def gathered_copies(array, axis, dim):
    return joined_along(sent_to_all(array, axis), dim)


def sum_by_axis(array, axes, dim):
    if not axes:
        return array
    nearer = lax.psum_scatter(array, axes[0], scatter_dimension=dim, tiled=True)
    return sum_by_axis(nearer, axes[1:], dim)


def build_target(positives, counts, start, width):
    columns = jnp.arange(width, dtype=jnp.int32)
    shifted = positives - start
    target = jnp.zeros((positives.shape[0], width), jnp.float32)
    for slot in range(positives.shape[1]):
        valid = counts > slot
        match = (shifted[:, slot][:, None] == columns[None, :]) & valid[:, None]
        target = target + match.astype(jnp.float32)
    return target


def per_device(queries, positives, counts, weight, master, moment_one, moment_two):
    rows = queries.shape[0]
    width = weight.shape[0]
    total = rows * lax.axis_size(DP)
    offset = lax.axis_index("label") * width
    whole = gathered_copies(queries, "label", 1)
    logits = lax.dot_general(
        whole, weight, (((1,), (1,)), ((), ())), preferred_element_type=jnp.float32
    )
    target = build_target(positives, counts, offset, width)
    grad_logit = ((jax.nn.sigmoid(logits) - target) / total).astype(jnp.bfloat16)
    full_grad = lax.dot_general(
        grad_logit, whole, (((0,), (0,)), ((), ())), preferred_element_type=jnp.float32
    )
    grad = sum_by_axis(full_grad, DP, 0)
    new_one = 0.9 * moment_one + 0.1 * grad
    new_two = 0.999 * moment_two + 0.001 * grad * grad
    first = new_one / (1.0 - 0.9**ADAM_STEP)
    second = new_two / (1.0 - 0.999**ADAM_STEP)
    new_master = master - 0.02 * (first / (jnp.sqrt(second) + 1e-08) + 0.01 * master)
    new_weight = gathered_copies(new_master.astype(jnp.bfloat16), DP, 0)
    return (new_weight, new_master, new_one, new_two)


def solution(mesh):
    torus = Mesh(mesh.devices.reshape(4, 8, mesh.shape["label"]), ("dp_0", "dp_1", "label"))
    in_specs = (
        P(DP, "label"),
        P(DP, None),
        P(DP),
        P("label", None),
        P(LABEL_DP, None),
        P(LABEL_DP, None),
        P(LABEL_DP, None),
    )
    out_specs = (P("label", None), P(LABEL_DP, None), P(LABEL_DP, None), P(LABEL_DP, None))
    return jax.shard_map(
        per_device, mesh=torus, in_specs=in_specs, out_specs=out_specs, check_vma=False
    )
```

profile of v0, /device:TPU:1, one launch (start us, length us, event | category | flops | bytes accessed | tf_op | source)
XLA Modules:
  0.0 315.0 jit_solution(10839794875244876992)
XLA Ops:
  7.2 0.0 copy-start
  7.2 0.0 copy-start.5
  7.2 0.0 copy-start.4
  7.2 2.1 broadcast_in_dim.4
  9.3 19.2 %all-to-all-start = ((bf16[16,512,64]{1,2,0:T(8,128)(2,1)}), bf16[16,512,64]{1,2,0:T(8,128)(2,1)S(1)}, u32[]{:S(2)}, u32[]{:S(2)}) async-start(bf16[16,512,64]{1,2,0:T(8,128)(2,1)} %broadcast_in_dim.4), calls=%async_computation | async-start | bytes 2097152 | tf_op jit(solution)/shard_map/all_to_all | solution.py:20
  28.5 0.0 reduce-scatter.3.cloned.1.call-start
  28.5 0.0 copy-done.5
  28.6 0.0 copy-done.4
  28.6 29.4 %all-to-all-done = bf16[16,512,64]{1,2,0:T(8,128)(2,1)S(1)} async-done(((bf16[16,512,64]{1,2,0:T(8,128)(2,1)}), bf16[16,512,64]{1,2,0:T(8,128)(2,1)S(1)}, u32[]{:S(2)}, u32[]{:S(2)}) %all-to-all-start) | async-done | bytes 1048608 | tf_op jit(solution)/shard_map/all_to_all | solution.py:20
  58.0 0.0 copy-done
  58.0 7.8 %fusion.8 = f32[1024,1024]{1,0:T(8,128)} fusion(bf16[512,1024]{0,1:T(8,128)(2,1)S(1)} %bitcast.16, bf16[1024,1024]{1,0:T(8,128)(2,1)S(1)} %copy-done, s32[512]{0:T(512)S(1)} %bitcast.18, s32[512]{0:T(512)S(1)} %bitcast.19, s32[512]{0:T(512)S(1)} %bitcast.20, s32[512]{0:T(512)S(1)} %bitcast.21, s32[512]{0:T(512)S(1)} %bitcast.22, s32[512]{0:T(512)S(1)} %bitcast.23, ...), kind=kOutput, calls=%fused_computation.17 | convolution fusion | flops 2166882304 | bytes 7360512 | tf_op jit(solution)/shard_map/dot_general | solution.py:58
  65.7 0.0 copy-start.1
  65.7 0.0 copy-start.2
  65.7 0.0 copy-start.3
  65.8 0.0 reduce-scatter.3.cloned.1.call-update
  65.8 0.0 reduce-scatter.5.cloned.1.call-start
  65.8 75.0 %reduce-scatter.3.cloned.1.call-done = f32[256,1024]{1,0:T(8,128)} async-done(((f32[1024,1024]{1,0:T(8,128)}), f32[256,1024]{1,0:T(8,128)}) %reduce-scatter.3.cloned.1.call-update) | async-done | bytes 1048592 | tf_op jit(solution)/shard_map/reduce_scatter | solution.py:32
  140.8 0.0 reduce-scatter.5.cloned.1.call-update
  140.8 65.0 %reduce-scatter.5.cloned.1.call-done = f32[32,1024]{1,0:T(8,128)} async-done(((f32[256,1024]{1,0:T(8,128)}), f32[32,1024]{1,0:T(8,128)}) %reduce-scatter.5.cloned.1.call-update) | async-done | bytes 131088 | tf_op jit(solution)/shard_map/reduce_scatter | solution.py:32
  205.9 0.0 copy-done.1
  205.9 0.0 copy-done.2
  205.9 0.0 copy-done.3
  205.9 1.7 fusion.30
  207.6 0.2 broadcast_in_dim.5
  207.9 99.0 %all_to_all.10 = bf16[32,32,1024]{2,1,0:T(8,128)(2,1)S(1)} all-to-all(bf16[32,32,1024]{2,1,0:T(8,128)(2,1)S(1)} %broadcast_in_dim.5), channel_id=1, replica_groups=mesh['dp_0'=4,'dp_1'=8,'label'=16] {'dp_0','dp_1'}, dimensions={0} | all-to-all | bytes 4194304 | tf_op jit(solution)/shard_map/all_to_all | solution.py:20
  306.9 1.3 copy.13
  (3 shorter events, 0.0 us)
Async XLA Ops:
  7.2 50.8 %copy-start = (bf16[1024,1024]{1,0:T(8,128)(2,1)S(1)}, bf16[1024,1024]{1,0:T(8,128)(2,1)}, u32[]{:S(2)}) copy-start(bf16[1024,1024]{1,0:T(8,128)(2,1)} %param.10) | copy-start | bytes 6291460
  7.2 21.4 %copy-start.5 = (s32[512]{0:T(512)S(1)}, s32[512]{0:T(512)}, u32[]{:S(2)}) copy-start(s32[512]{0:T(512)} %param.9) | copy-start | bytes 6148
  7.2 21.4 %copy-start.4 = (s32[512,8]{0,1:T(8,128)S(1)}, s32[512,8]{0,1:T(8,128)}, u32[]{:S(2)}) copy-start(s32[512,8]{0,1:T(8,128)} %param.8) | copy-start | bytes 49156
  9.3 48.7 %all-to-all-start = ((bf16[16,512,64]{1,2,0:T(8,128)(2,1)}), bf16[16,512,64]{1,2,0:T(8,128)(2,1)S(1)}, u32[]{:S(2)}, u32[]{:S(2)}) async-start(bf16[16,512,64]{1,2,0:T(8,128)(2,1)} %broadcast_in_dim.4), calls=%async_computation | async-start | bytes 2097152 | tf_op jit(solution)/shard_map/all_to_all | solution.py:20
  28.5 112.3 %reduce-scatter.3.cloned.1.call-start = ((), (), s32[]{:S(2)}) async-start(), calls=%async_computation.4 | async-start | bytes 5242880 | tf_op jit(solution)/shard_map/reduce_scatter | solution.py:32
  65.7 140.2 %copy-start.1 = (f32[32,1024]{1,0:T(8,128)S(1)}, f32[32,1024]{1,0:T(8,128)}, u32[]{:S(2)}) copy-start(f32[32,1024]{1,0:T(8,128)} %param.11) | copy-start | bytes 393220
  65.7 140.2 %copy-start.2 = (f32[32,1024]{1,0:T(8,128)S(1)}, f32[32,1024]{1,0:T(8,128)}, u32[]{:S(2)}) copy-start(f32[32,1024]{1,0:T(8,128)} %param.12) | copy-start | bytes 393220
  65.7 140.2 %copy-start.3 = (f32[32,1024]{1,0:T(8,128)S(1)}, f32[32,1024]{1,0:T(8,128)}, u32[]{:S(2)}) copy-start(f32[32,1024]{1,0:T(8,128)} %param.13) | copy-start | bytes 393220
  65.8 140.1 %reduce-scatter.5.cloned.1.call-start = ((), (), s32[]{:S(2)}) async-start(), calls=%async_computation.5 | async-start | bytes 1179648 | tf_op jit(solution)/shard_map/reduce_scatter | solution.py:32
Sparse Core Ops, SparseCore 0:
  65.9 74.8 reduce-scatter.2
  143.6 62.2 reduce-scatter.4
where the time goes:
time: 319 us; the launch traced here: 315 us
  waiting for transfers between devices  169 us (53%)
  blocking collectives  99 us (31%)
  starting transfers between devices  19.3 us (6%)
  between operations  14.1 us (4%)
  matrix products  7.77 us (2%)
  local copies, waits for them, and re-layouts  3.67 us (1%)
    reduce_scatter x2, waiting for transfers between devices, sum_by_axis(): nearer = lax.psum_scatter(array, axes[0], scatter_dimension=dim, tiled=True)  140 us
    all_to_all x1, blocking collectives, sent_to_all(): lax.all_to_all(jnp.broadcast_to(array[None], (count, *array.shape)), axis...  99 us
    all_to_all x1, waiting for transfers between devices, sent_to_all(): lax.all_to_all(jnp.broadcast_to(array[None], (count, *array.shape)), axis...  29.4 us
    all_to_all x1, starting transfers between devices, sent_to_all(): lax.all_to_all(jnp.broadcast_to(array[None], (count, *array.shape)), axis...  19.2 us
    dot_general x1, matrix products, per_device(): lax.dot_general(grad_logit, whole, (((0,), (0,)), ((), ())), preferred_el...  7.77 us
  transfers between devices with their start and end apart: 3, of which 3 were waited for; matrix products, arithmetic and copies ran while one was open for 0% of the time, Pallas kernels for 0%

commit v1 on v0

v1 whole, which is shorter than its diff:
```python
import jax
import jax.numpy as jnp
from jax import lax
from jax.experimental import pallas as pl
from jax.experimental.pallas import tpu as pltpu
from jax.sharding import Mesh
from jax.sharding import PartitionSpec as P

ADAM_STEP = 10
AXES = ("x", "zq", "zp", "y", "zh", "c")
DP = ("x", "zq", "zp")
LABEL = ("y", "zh", "c")
SWAP = [(0, 1), (1, 0)]


def grad_kernel(where, own, other, pos_own, pos_other, weight, out, whole, ids):
    core, pair, first_label = where[0], where[1], where[2]
    spans, runs, feats, block = own.shape[0], own.shape[1], own.shape[2], own.shape[3]
    run_count = weight.shape[0]
    run_rows = weight.shape[2]
    rows = run_count * run_rows
    for span in range(spans):
        for run in range(runs):
            at = run * 2 * feats
            whole[span, pl.ds(pl.multiple_of(at + core * feats, feats), feats), :] = own[span, run]
            whole[span, pl.ds(pl.multiple_of(at + (1 - core) * feats, feats), feats), :] = other[span, run]
    ids[pl.ds(pair, 1)] = pos_own[...][None]
    ids[pl.ds(1 - pair, 1)] = pos_other[...][None]
    rows_w = weight[...].reshape(rows, weight.shape[3])
    row = lax.broadcasted_iota(jnp.int32, (rows, 1), 0)
    label = first_label + (row // run_rows) * (2 * run_rows) + row % run_rows
    total = None
    for span in range(spans):
        block_q = whole[span]
        logits = jnp.dot(rows_w, block_q, preferred_element_type=jnp.float32)
        hit = label == ids[span, 0:1, :]
        for slot in range(1, ids.shape[1]):
            hit = hit | (label == ids[span, slot : slot + 1, :])
        diff = jax.nn.sigmoid(logits) - hit.astype(jnp.float32)
        grad_logit = (diff * (1.0 / 16384)).astype(jnp.bfloat16)
        part = lax.dot_general(
            grad_logit, block_q, (((1,), (1,)), ((), ())), preferred_element_type=jnp.float32
        )
        total = part if total is None else total + part
    out[...] = total.astype(jnp.bfloat16)


def summed(terms):
    total = terms[0].astype(jnp.float32)
    for term in range(1, terms.shape[0]):
        total = total + terms[term].astype(jnp.float32)
    return total


def per_device(queries, positives, counts, weight, master, moment_one, moment_two):
    local_q, feats = queries.shape
    labels, width = weight.shape
    own_rows = master.shape[0]
    x_n, zq_n, zp_n = (lax.axis_size(a) for a in DP)
    y_n, zh_n, c_n = (lax.axis_size(a) for a in LABEL)
    core, pair, half = lax.axis_index("c"), lax.axis_index("zp"), lax.axis_index("zh")

    mine = queries.T
    far = lax.ppermute(mine, "zh", SWAP)
    slots = lax.broadcasted_iota(jnp.int32, (positives.shape[1], local_q), 0)
    ids_own = jnp.where(slots < counts[None, :], positives.T, -1)
    ids_other = lax.ppermute(ids_own, "zp", SWAP)

    both = jnp.where(half == 0, jnp.stack([mine, far]), jnp.stack([far, mine]))
    sent = jnp.broadcast_to(both[None], (y_n * zp_n, *both.shape))
    got = lax.all_to_all(sent, ("zp", "y"), 0, 0, tiled=True)
    got = got.reshape(zp_n, y_n * zh_n, feats, local_q)
    got_other = lax.ppermute(got, "c", SWAP)

    runs = weight.reshape(x_n * zq_n, zp_n, own_rows, width)
    rows_w = lax.dynamic_slice_in_dim(runs, pair, 1, 1)
    label_block = lax.axis_index(LABEL)
    first = label_block * labels + pair * own_rows
    where = jnp.stack([core, pair, first]).astype(jnp.int32)
    rows = x_n * zq_n * own_rows
    vmem = pl.BlockSpec(memory_space=pltpu.VMEM)
    part = pl.pallas_call(
        grad_kernel,
        out_shape=jax.ShapeDtypeStruct((rows, width), jnp.bfloat16),
        in_specs=[pl.BlockSpec(memory_space=pltpu.SMEM)] + [vmem] * 5,
        out_specs=vmem,
        scratch_shapes=[
            pltpu.VMEM((zp_n, width, local_q), jnp.bfloat16),
            pltpu.VMEM((zp_n, positives.shape[1], local_q), jnp.int32),
        ],
        cost_estimate=pl.CostEstimate(
            flops=4 * rows * width * zp_n * local_q, bytes_accessed=6 << 20, transcendentals=0
        ),
    )(where, got, got_other, ids_own, ids_other, rows_w)

    by_x = lax.all_to_all(part.reshape(x_n, zq_n * own_rows, width), "x", 0, 0, tiled=True)
    by_x = summed(by_x).astype(jnp.bfloat16)
    by_z = lax.all_to_all(by_x.reshape(zq_n, own_rows, width), "zq", 0, 0, tiled=True)
    grad = summed(by_z)

    new_one = 0.9 * moment_one + 0.1 * grad
    new_two = 0.999 * moment_two + 0.001 * grad * grad
    first = new_one / (1.0 - 0.9**ADAM_STEP)
    second = new_two / (1.0 - 0.999**ADAM_STEP)
    new_master = master - 0.02 * (first / (jnp.sqrt(second) + 1e-08) + 0.01 * master)
    low = new_master.astype(jnp.bfloat16)

    along_z = lax.all_to_all(
        jnp.broadcast_to(low[None], (zq_n, own_rows, width)), "zq", 0, 0, tiled=True
    )
    everywhere = lax.all_to_all(
        jnp.broadcast_to(along_z[None], (x_n * zp_n, zq_n, own_rows, width)),
        ("x", "zp"), 0, 0, tiled=True,
    )
    everywhere = everywhere.reshape(x_n, zp_n, zq_n, own_rows, width)
    new_weight = everywhere.transpose(0, 2, 1, 3, 4).reshape(labels, width)
    return (new_weight, new_master, new_one, new_two)


def solution(mesh):
    torus = Mesh(mesh.devices.reshape(4, 4, 2, 4, 2, 2), AXES)
    in_specs = (
        P(DP, LABEL),
        P(DP, None),
        P(DP),
        P(LABEL, None),
        P(LABEL + DP, None),
        P(LABEL + DP, None),
        P(LABEL + DP, None),
    )
    out_specs = (P(LABEL, None),) + (P(LABEL + DP, None),) * 3
    return jax.shard_map(
        per_device, mesh=torus, in_specs=in_specs, out_specs=out_specs, check_vma=False
    )
```

time: 319 us -> 151 us (0.47); the launches traced: 315 us -> 151 us
  waiting for transfers between devices: 169 us -> 2.53 us
  between operations: 14.1 us -> 0.8 us
  blocking collectives: 99 us -> 110 us
  matrix products: 7.77 us -> 0 us
  Pallas kernels: 0 us -> 6.31 us
  starting transfers between devices: 19.3 us -> 25.5 us
    reduce_scatter x2 -> x0, waiting for transfers between devices: 140 us -> none  [sum_by_axis(): nearer = lax.psum_scatter(array, axes[0], scatter_dimension=dim, tiled=True)]
    all_to_all x1 -> x0, waiting for transfers between devices: 29.4 us -> none  [sent_to_all(): lax.all_to_all(jnp.broadcast_to(array[None], (count, *array.shape)), axis...]
    ppermute x0 -> x3, starting transfers between devices: none -> 25.5 us  [the longest x1 16.4 us: per_device(): far = lax.ppermute(mine, 'zh', SWAP)]
    all_to_all x1 -> x0, starting transfers between devices: 19.2 us -> none  [sent_to_all(): lax.all_to_all(jnp.broadcast_to(array[None], (count, *array.shape)), axis...]
    all_to_all x1 -> x5, blocking collectives: 99 us -> 110 us  [the longest x1 36.1 us: per_device(): lax.all_to_all(jnp.broadcast_to(along_z[None], (x_n * zp_n, zq_n, own_row...]
    dot_general x1 -> x0, matrix products: 7.77 us -> none  [per_device(): lax.dot_general(grad_logit, whole, (((0,), (0,)), ((), ())), preferred_el...]
    pallas_call x0 -> x1, Pallas kernels: none -> 6.31 us  [per_device(): pl.pallas_call(grad_kernel, out_shape=jax.ShapeDtypeStruct((rows, width),...]
  transfers between devices with their start and end apart: 3 -> 3, of which waited for: 3 -> 2; matrix products, arithmetic and copies ran while one was open for 0% -> 1% of each run, Pallas kernels for 0% -> 0%
where the time goes in v1:
time: 151 us
  blocking collectives  110 us (73%)
  starting transfers between devices  25.5 us (17%)
  Pallas kernels  6.31 us (4%)
  local copies, waits for them, and re-layouts  3.58 us (2%)
  other arithmetic  2.55 us (2%)
  waiting for transfers between devices  2.53 us (2%)
    all_to_all x1, blocking collectives, per_device(): lax.all_to_all(jnp.broadcast_to(along_z[None], (x_n * zp_n, zq_n, own_row...  36.1 us
    all_to_all x1, blocking collectives, per_device(): lax.all_to_all(by_x.reshape(zq_n, own_rows, width), 'zq', 0, 0, tiled=True)  26 us
    all_to_all x1, blocking collectives, per_device(): lax.all_to_all(part.reshape(x_n, zq_n * own_rows, width), 'x', 0, 0, tile...  17.6 us
    ppermute x1, starting transfers between devices, per_device(): far = lax.ppermute(mine, 'zh', SWAP)  16.4 us
    all_to_all x1, blocking collectives, per_device(): got = lax.all_to_all(sent, ('zp', 'y'), 0, 0, tiled=True)  15.9 us
    all_to_all x1, blocking collectives, per_device(): lax.all_to_all(jnp.broadcast_to(low[None], (zq_n, own_rows, width)), 'zq'...  14.2 us
    ppermute x1, starting transfers between devices, per_device(): got_other = lax.ppermute(got, 'c', SWAP)  6.86 us
    pallas_call x1, Pallas kernels, per_device(): pl.pallas_call(grad_kernel, out_shape=jax.ShapeDtypeStruct((rows, width),...  6.31 us
  transfers between devices with their start and end apart: 3, of which 2 were waited for; matrix products, arithmetic and copies ran while one was open for 1% of the time, Pallas kernels for 0%

profile of v1, /device:TPU:1, one launch (start us, length us, event | category | flops | bytes accessed | tf_op | source)
XLA Modules:
  0.0 151.0 jit_solution(2614090839855019635)
XLA Ops:
  0.6 0.0 copy-start
  0.6 0.0 copy-start.7
  0.7 0.0 copy-start.5
  0.7 16.4 %collective-permute-start = (bf16[64,512]{1,0:T(8,128)(2,1)}, bf16[64,512]{1,0:T(8,128)(2,1)S(1)}, u32[]{:S(2)}, u32[]{:S(2)}) collective-permute-start(bf16[64,512]{1,0:T(8,128)(2,1)} %bitcast.31), channel_id=1, source_target_pairs={{0,2},{2,0},{1,3},{3,1},{4,6},{6,4},{5,7},{7,5},{8,10},{10,8},{9,1... | collective-permute-start | bytes 196616 | tf_op jit(solution)/shard_map/ppermute | solution.py:64
  17.1 2.0 %collective-permute-done = bf16[64,512]{1,0:T(8,128)(2,1)S(1)} collective-permute-done((bf16[64,512]{1,0:T(8,128)(2,1)}, bf16[64,512]{1,0:T(8,128)(2,1)S(1)}, u32[]{:S(2)}, u32[]{:S(2)}) %collective-permute-start) | collective-permute-done | bytes 65568 | tf_op jit(solution)/shard_map/ppermute | solution.py:64
  19.1 0.9 maximum_select_fusion
  20.1 0.1 broadcast_in_dim.10
  20.2 15.9 %all_to_all.25 = bf16[8,2,64,512]{3,2,1,0:T(8,128)(2,1)S(1)} all-to-all(bf16[8,2,64,512]{3,2,1,0:T(8,128)(2,1)S(1)} %broadcast_in_dim.10), channel_id=1, replica_groups=mesh['x'=4,'zq'=4,'zp'=2,'y'=4,'zh'=2,'c'=2] {'zp','y'}, dimensions={0} | all-to-all | bytes 2097152 | tf_op jit(solution)/shard_map/all_to_all | solution.py:71
  36.0 0.0 copy-start.1
  36.0 6.9 %collective-permute-start.1 = (bf16[2,8,64,512]{3,2,1,0:T(8,128)(2,1)S(1)}, bf16[2,8,64,512]{3,2,1,0:T(8,128)(2,1)}, u32[]{:S(2)}, u32[]{:S(2)}) collective-permute-start(bf16[2,8,64,512]{3,2,1,0:T(8,128)(2,1)S(1)} %bitcast.28), channel_id=1, source_target_pairs={{0,1},{1,0},{2,3},{3,2},{4,5},{5,4},{6,7},{7,6},{8,9},{9,8},{10,11... | collective-permute-start | bytes 3145736 | tf_op jit(solution)/shard_map/ppermute | solution.py:73
  42.9 0.0 copy-done.7
  42.9 0.0 copy-done.5
  42.9 0.0 copy-start.6
  42.9 2.3 %collective-permute-start.2 = (s32[8,512]{1,0:T(8,128)S(1)}, s32[8,512]{1,0:T(8,128)S(1)}, u32[]{:S(2)}, u32[]{:S(2)}) collective-permute-start(s32[8,512]{1,0:T(8,128)S(1)} %bitcast_select_fusion.pos_own), channel_id=1, source_target_pairs={{0,16},{16,0},{1,17},{17,1},{2,18},{18,2},{3,19},{19,3},{4,20},{20... | collective-permute-start | bytes 49160 | tf_op jit(solution)/shard_map/ppermute | solution.py:67
  45.2 0.0 copy-done
  45.2 1.1 constant_dynamic-slice_fusion.weight
  46.3 0.6 pad_add_fusion.where
  47.0 0.5 collective-permute-done.2.pos_other
  47.4 0.0 copy-start.8
  47.4 0.0 collective-permute-done.1.other
  47.4 0.0 copy-done.1
  47.4 0.0 copy-done.6
  47.5 0.6 copy-done.8
  48.0 6.3 %shard_map.102 = bf16[512,1024]{1,0:T(8,128)(2,1)} custom-call(s32[3]{0:T(128)} %pad_add_fusion.where, bf16[2,8,64,512]{3,2,1,0:T(8,128)(2,1)} %bitcast.29, bf16[2,8,64,512]{3,2,1,0:T(8,128)(2,1)} %collective-permute-done.1.other, s32[8,512]{1,0:T(8,128)} %copy-done.6, s32[8,512]{1,0:T(8,128)} %copy-done.8, ...), custom_call_target="tpu_custom_call" | custom-call | flops 2147483648 | bytes 6291456 | tf_op jit(solution)/shard_map/pallas_call | solution.py:82
  54.4 0.0 copy-start.2
  54.4 0.0 copy-start.3
  54.4 0.0 copy-start.4
  54.4 17.6 %all_to_all.26 = bf16[4,128,1024]{2,1,0:T(8,128)(2,1)S(1)} all-to-all(bf16[4,128,1024]{2,1,0:T(8,128)(2,1)} %bitcast.30), channel_id=1, replica_groups=mesh['x'=4,'zq'=4,'zp'=2,'y'=4,'zh'=2,'c'=2] {'x'}, dimensions={0} | all-to-all | bytes 2097152 | tf_op jit(solution)/shard_map/all_to_all | solution.py:96
  72.0 0.2 add_convert_fusion
  72.1 26.0 %all_to_all.27 = bf16[4,32,1024]{2,1,0:T(8,128)(2,1)S(1)} all-to-all(bf16[4,32,1024]{2,1,0:T(8,128)(2,1)S(1)} %bitcast.27), channel_id=1, replica_groups=mesh['x'=4,'zq'=4,'zp'=2,'y'=4,'zh'=2,'c'=2] {'zq'}, dimensions={0} | all-to-all | bytes 524288 | tf_op jit(solution)/shard_map/all_to_all | solution.py:98
  98.1 0.0 copy-done.2
  98.1 0.0 copy-done.3
  98.1 0.0 copy-done.4
  98.1 0.8 fusion.2
  99.0 14.2 %all_to_all.28 = bf16[4,32,1024]{2,1,0:T(8,128)(2,1)S(1)} all-to-all(bf16[4,32,1024]{2,1,0:T(8,128)(2,1)S(1)} %broadcast_in_dim.12), channel_id=1, replica_groups=mesh['x'=4,'zq'=4,'zp'=2,'y'=4,'zh'=2,'c'=2] {'zq'}, dimensions={0} | all-to-all | bytes 524288 | tf_op jit(solution)/shard_map/all_to_all | solution.py:108
  113.1 0.3 broadcast_in_dim.13
  113.4 36.1 %all_to_all.29 = bf16[8,4,32,1024]{3,2,1,0:T(8,128)(2,1)S(1)} all-to-all(bf16[8,4,32,1024]{3,2,1,0:T(8,128)(2,1)S(1)} %broadcast_in_dim.13), channel_id=1, replica_groups=mesh['x'=4,'zq'=4,'zp'=2,'y'=4,'zh'=2,'c'=2] {'x','zp'}, dimensions={0} | all-to-all | bytes 4194304 | tf_op jit(solution)/shard_map/all_to_all | solution.py:111
  149.5 1.5 copy.11
  (2 shorter events, 0.0 us)
Async XLA Ops:
  0.6 44.6 %copy-start = (bf16[1024,1024]{1,0:T(8,128)(2,1)S(1)}, bf16[1024,1024]{1,0:T(8,128)(2,1)}, u32[]{:S(2)}) copy-start(bf16[1024,1024]{1,0:T(8,128)(2,1)} %param.10) | copy-start | bytes 6291460
  0.6 42.3 %copy-start.7 = (s32[512]{0:T(512)S(1)}, s32[512]{0:T(512)}, u32[]{:S(2)}) copy-start(s32[512]{0:T(512)} %param.9) | copy-start | bytes 6148
  0.7 42.3 %copy-start.5 = (s32[512,8]{0,1:T(8,128)S(1)}, s32[512,8]{0,1:T(8,128)}, u32[]{:S(2)}) copy-start(s32[512,8]{0,1:T(8,128)} %param.8) | copy-start | bytes 49156
  0.7 18.5 %collective-permute-start = (bf16[64,512]{1,0:T(8,128)(2,1)}, bf16[64,512]{1,0:T(8,128)(2,1)S(1)}, u32[]{:S(2)}, u32[]{:S(2)}) collective-permute-start(bf16[64,512]{1,0:T(8,128)(2,1)} %bitcast.31), channel_id=1, source_target_pairs={{0,2},{2,0},{1,3},{3,1},{4,6},{6,4},{5,7},{7,5},{8,10},{10,8},{9,1... | collective-permute-start | bytes 196616 | tf_op jit(solution)/shard_map/ppermute | solution.py:64
  36.0 11.4 %copy-start.1 = (bf16[8,2,64,512]{3,2,1,0:T(8,128)(2,1)}, bf16[8,2,64,512]{3,2,1,0:T(8,128)(2,1)S(1)}, u32[]{:S(2)}) copy-start(bf16[8,2,64,512]{3,2,1,0:T(8,128)(2,1)S(1)} %all_to_all.25) | copy-start | bytes 3145732
  36.0 11.4 %collective-permute-start.1 = (bf16[2,8,64,512]{3,2,1,0:T(8,128)(2,1)S(1)}, bf16[2,8,64,512]{3,2,1,0:T(8,128)(2,1)}, u32[]{:S(2)}, u32[]{:S(2)}) collective-permute-start(bf16[2,8,64,512]{3,2,1,0:T(8,128)(2,1)S(1)} %bitcast.28), channel_id=1, source_target_pairs={{0,1},{1,0},{2,3},{3,2},{4,5},{5,4},{6,7},{7,6},{8,9},{9,8},{10,11... | collective-permute-start | bytes 3145736 | tf_op jit(solution)/shard_map/ppermute | solution.py:73
  42.9 4.5 %copy-start.6 = (s32[8,512]{1,0:T(8,128)}, s32[8,512]{1,0:T(8,128)S(1)}, u32[]{:S(2)}) copy-start(s32[8,512]{1,0:T(8,128)S(1)} %bitcast_select_fusion.pos_own) | copy-start | bytes 49156
  42.9 4.5 %collective-permute-start.2 = (s32[8,512]{1,0:T(8,128)S(1)}, s32[8,512]{1,0:T(8,128)S(1)}, u32[]{:S(2)}, u32[]{:S(2)}) collective-permute-start(s32[8,512]{1,0:T(8,128)S(1)} %bitcast_select_fusion.pos_own), channel_id=1, source_target_pairs={{0,16},{16,0},{1,17},{17,1},{2,18},{18,2},{3,19},{19,3},{4,20},{20... | collective-permute-start | bytes 49160 | tf_op jit(solution)/shard_map/ppermute | solution.py:67
  47.4 0.6 copy-start.8
  54.4 43.8 %copy-start.2 = (f32[32,1024]{1,0:T(8,128)S(1)}, f32[32,1024]{1,0:T(8,128)}, u32[]{:S(2)}) copy-start(f32[32,1024]{1,0:T(8,128)} %param.11) | copy-start | bytes 393220
  54.4 43.8 %copy-start.3 = (f32[32,1024]{1,0:T(8,128)S(1)}, f32[32,1024]{1,0:T(8,128)}, u32[]{:S(2)}) copy-start(f32[32,1024]{1,0:T(8,128)} %param.12) | copy-start | bytes 393220
  54.4 43.8 %copy-start.4 = (f32[32,1024]{1,0:T(8,128)S(1)}, f32[32,1024]{1,0:T(8,128)}, u32[]{:S(2)}) copy-start(f32[32,1024]{1,0:T(8,128)} %param.13) | copy-start | bytes 393220

commit v2 on v1

v2 whole, which is shorter than its diff:
```python
import jax
import jax.numpy as jnp
from jax import lax
from jax.experimental import pallas as pl
from jax.experimental.pallas import tpu as pltpu
from jax.sharding import Mesh
from jax.sharding import PartitionSpec as P

ADAM_STEP = 10
AXES = ("x", "zf", "zm", "zp", "y", "zh", "c")
DP = ("x", "zf", "zm", "zp")
LABEL = ("y", "zh", "c")
SWAP = [(0, 1), (1, 0)]


def grad_kernel(where, own, other, ids_own, ids_far, weight, out, whole, ids):
    core, far, first_label = where[0], where[1], where[2]
    ys, blocks, halves, feats = own.shape[:4]
    runs, _, run_rows, width = weight.shape
    rows = runs * run_rows
    for y in range(ys):
        for block in range(blocks):
            for half in range(halves):
                at = (y * halves + half) * 2 * feats
                mine = pl.ds(pl.multiple_of(at + core * feats, feats), feats)
                theirs = pl.ds(pl.multiple_of(at + (1 - core) * feats, feats), feats)
                whole[block, mine, :] = own[y, block, half]
                whole[block, theirs, :] = other[y, block, half]
    ids[pl.ds(far, 1)] = ids_own[...][None]
    ids[pl.ds(1 - far, 1)] = ids_far[...][None]
    rows_w = weight[...].reshape(rows, width)
    row = lax.broadcasted_iota(jnp.int32, (rows, 1), 0)
    label = first_label + (row // run_rows) * (2 * run_rows) + row % run_rows
    total = None
    for block in range(blocks):
        block_q = whole[block]
        logits = jnp.dot(rows_w, block_q, preferred_element_type=jnp.float32)
        hit = label == ids[block, 0:1, :]
        for slot in range(1, ids.shape[1]):
            hit = hit | (label == ids[block, slot : slot + 1, :])
        diff = jax.nn.sigmoid(logits) - hit.astype(jnp.float32)
        grad_logit = (diff * (1.0 / 16384)).astype(jnp.bfloat16)
        part = lax.dot_general(
            grad_logit, block_q, (((1,), (1,)), ((), ())), preferred_element_type=jnp.float32
        )
        total = part if total is None else total + part
    out[...] = total.astype(jnp.bfloat16)


def summed(terms):
    total = terms[0].astype(jnp.float32)
    for term in range(1, terms.shape[0]):
        total = total + terms[term].astype(jnp.float32)
    return total


def to_all(array, axes):
    count = lax.axis_size(axes)
    return lax.all_to_all(
        jnp.broadcast_to(array[None], (count, *array.shape)), axes, 0, 0, tiled=True
    )


def per_device(queries, positives, counts, weight, master, moment_one, moment_two):
    local_q, feats = queries.shape
    labels, width = weight.shape
    own_rows = master.shape[0]
    x_n, zf_n, zm_n, zp_n = (lax.axis_size(a) for a in DP)
    y_n, zh_n, c_n = (lax.axis_size(a) for a in LABEL)
    core, far = lax.axis_index("c"), lax.axis_index("zf")
    near_rows = zm_n * zp_n * own_rows
    rows = x_n * near_rows

    slots = lax.broadcasted_iota(jnp.int32, (positives.shape[1], local_q), 0)
    ids_own = jnp.where(slots < counts[None, :], positives.T, -1)
    ids_far = lax.ppermute(ids_own, "zf", SWAP)

    along_z = to_all(queries.T, ("zf", "zh"))
    along_y = to_all(along_z.reshape(zf_n, zh_n, feats, local_q), "y")
    other = lax.ppermute(along_y, "c", SWAP)

    runs = weight.reshape(x_n, zf_n, near_rows, width)
    rows_w = lax.dynamic_slice_in_dim(runs, far, 1, 1)
    first = lax.axis_index(LABEL) * labels + far * near_rows
    where = jnp.stack([core, far, first]).astype(jnp.int32)
    vmem = pl.BlockSpec(memory_space=pltpu.VMEM)
    part = pl.pallas_call(
        grad_kernel,
        out_shape=jax.ShapeDtypeStruct((rows, width), jnp.bfloat16),
        in_specs=[pl.BlockSpec(memory_space=pltpu.SMEM)] + [vmem] * 5,
        out_specs=vmem,
        scratch_shapes=[
            pltpu.VMEM((zf_n, width, local_q), jnp.bfloat16),
            pltpu.VMEM((zf_n, positives.shape[1], local_q), jnp.int32),
        ],
        cost_estimate=pl.CostEstimate(
            flops=4 * rows * width * zf_n * local_q, bytes_accessed=6 << 20, transcendentals=0
        ),
    )(where, along_y, other, ids_own, ids_far, rows_w)

    owners = x_n * zm_n * zp_n
    terms = lax.all_to_all(
        part.reshape(owners, own_rows, width), ("x", "zm", "zp"), 0, 0, tiled=True
    )
    grad = summed(terms)

    new_one = 0.9 * moment_one + 0.1 * grad
    new_two = 0.999 * moment_two + 0.001 * grad * grad
    first = new_one / (1.0 - 0.9**ADAM_STEP)
    second = new_two / (1.0 - 0.999**ADAM_STEP)
    new_master = master - 0.02 * (first / (jnp.sqrt(second) + 1e-08) + 0.01 * master)
    low = new_master.astype(jnp.bfloat16)

    every = to_all(to_all(low, ("zf", "zm")), ("x", "zp"))
    every = every.reshape(x_n, zp_n, zf_n * zm_n, own_rows, width)
    new_weight = every.transpose(0, 2, 1, 3, 4).reshape(labels, width)
    return (new_weight, new_master, new_one, new_two)


def solution(mesh):
    torus = Mesh(mesh.devices.reshape(4, 2, 2, 2, 4, 2, 2), AXES)
    in_specs = (
        P(DP, LABEL),
        P(DP, None),
        P(DP),
        P(LABEL, None),
        P(LABEL + DP, None),
        P(LABEL + DP, None),
        P(LABEL + DP, None),
    )
    out_specs = (P(LABEL, None),) + (P(LABEL + DP, None),) * 3
    return jax.shard_map(
        per_device, mesh=torus, in_specs=in_specs, out_specs=out_specs, check_vma=False
    )
```

time: 151 us -> 158 us (1.046)
  blocking collectives: 110 us -> 127 us
  starting transfers between devices: 25.5 us -> 15.5 us
    all_to_all x5, blocking collectives: 110 us -> 127 us  [the longest x4 88.1 us: to_all(): lax.all_to_all(jnp.broadcast_to(array[None], (count, *array.shape)), axes...]
    ppermute x3 -> x2, starting transfers between devices: 25.5 us -> 15.5 us  [the longest x1 9.89 us: per_device(): other = lax.ppermute(along_y, 'c', SWAP)]
  transfers between devices with their start and end apart: 3 -> 2, of which waited for: 2 -> 1; matrix products, arithmetic and copies ran while one was open for 1% -> 1% of each run, Pallas kernels for 0% -> 0%
where the time goes in v2:
time: 158 us; the launch traced here: 157 us
  blocking collectives  127 us (80%)
  starting transfers between devices  15.5 us (10%)
  Pallas kernels  6.33 us (4%)
  local copies, waits for them, and re-layouts  4.56 us (3%)
  other arithmetic  1.63 us (1%)
    all_to_all x4, blocking collectives, to_all(): lax.all_to_all(jnp.broadcast_to(array[None], (count, *array.shape)), axes...  88.1 us
    all_to_all x1, blocking collectives, per_device(): lax.all_to_all(part.reshape(owners, own_rows, width), ('x', 'zm', 'zp'),...  38.7 us
    ppermute x1, starting transfers between devices, per_device(): other = lax.ppermute(along_y, 'c', SWAP)  9.89 us
    pallas_call x1, Pallas kernels, per_device(): pl.pallas_call(grad_kernel, out_shape=jax.ShapeDtypeStruct((rows, width),...  6.33 us
    ppermute x1, starting transfers between devices, per_device(): ids_far = lax.ppermute(ids_own, 'zf', SWAP)  5.59 us
  transfers between devices with their start and end apart: 2, of which 1 were waited for; matrix products, arithmetic and copies ran while one was open for 1% of the time, Pallas kernels for 0%

profile of v2, /device:TPU:1, one launch (start us, length us, event | category | flops | bytes accessed | tf_op | source)
XLA Modules:
  0.0 156.7 jit_solution(12511402372437737101)
XLA Ops:
  0.6 0.0 copy-start
  0.6 0.0 copy-start.5
  0.7 0.0 copy-start.7
  0.7 1.0 broadcast_in_dim.14
  1.7 28.6 %all_to_all.25 = bf16[4,64,512]{2,1,0:T(8,128)(2,1)S(1)} all-to-all(bf16[4,64,512]{2,1,0:T(8,128)(2,1)S(1)} %broadcast_in_dim.14), channel_id=1, replica_groups=mesh['x'=4,'zf'=2,'zm'=2,'zp'=2,'y'=4,'zh'=2,'c'=2] {'zf','zh'}, dimensions={0} | all-to-all | bytes 524288 | tf_op jit(solution)/shard_map/all_to_all | solution.py:59
  30.2 0.1 broadcast_in_dim.16
  30.3 13.7 %all_to_all.26.own = bf16[4,2,2,64,512]{4,3,2,1,0:T(8,128)(2,1)S(1)} all-to-all(bf16[4,2,2,64,512]{4,3,2,1,0:T(8,128)(2,1)S(1)} %broadcast_in_dim.16), channel_id=1, replica_groups=mesh['x'=4,'zf'=2,'zm'=2,'zp'=2,'y'=4,'zh'=2,'c'=2] {'y'}, dimensions={0} | all-to-all | bytes 2097152 | tf_op jit(solution)/shard_map/all_to_all | solution.py:59
  44.1 0.0 copy-start.1
  44.1 9.9 %collective-permute-start = (bf16[4,2,2,64,512]{4,3,2,1,0:T(8,128)(2,1)S(1)}, bf16[4,2,2,64,512]{4,3,2,1,0:T(8,128)(2,1)}, u32[]{:S(2)}, u32[]{:S(2)}) collective-permute-start(bf16[4,2,2,64,512]{4,3,2,1,0:T(8,128)(2,1)S(1)} %all_to_all.26.own), channel_id=1, source_target_pairs={{0,1},{1,0},{2,3},{3,2},{4,5},{5,4},{6,7},{7,6},{8,9},{9,8},{10,11... | collective-permute-start | bytes 3145736 | tf_op jit(solution)/shard_map/ppermute | solution.py:80
  54.0 0.0 copy-done.5
  54.0 0.0 copy-done.7
  54.0 0.0 copy-start.6
  54.0 5.6 %collective-permute-start.1 = (s32[8,512]{1,0:T(8,128)S(1)}, s32[8,512]{1,0:T(8,128)S(1)}, u32[]{:S(2)}, u32[]{:S(2)}) collective-permute-start(s32[8,512]{1,0:T(8,128)S(1)} %bitcast_select_fusion.ids_own), channel_id=1, source_target_pairs={{0,64},{64,0},{1,65},{65,1},{2,66},{66,2},{3,67},{67,3},{4,68},{68... | collective-permute-start | bytes 49160 | tf_op jit(solution)/shard_map/ppermute | solution.py:76
  59.6 0.0 copy-done
  59.6 1.1 constant_dynamic-slice_fusion.weight
  60.7 0.7 pad_add_fusion.where
  61.3 1.0 collective-permute-done.1.ids_far
  62.4 0.0 copy-start.8
  62.4 0.0 collective-permute-done.other
  62.4 0.0 copy-done.1
  62.4 0.0 copy-done.6
  62.4 0.6 copy-done.8
  63.0 6.3 %shard_map.102 = bf16[512,1024]{1,0:T(8,128)(2,1)} custom-call(s32[3]{0:T(128)} %pad_add_fusion.where, bf16[4,2,2,64,512]{4,3,2,1,0:T(8,128)(2,1)} %copy-done.1, bf16[4,2,2,64,512]{4,3,2,1,0:T(8,128)(2,1)} %collective-permute-done.other, s32[8,512]{1,0:T(8,128)} %copy-done.6, s32[8,512]{1,0:T(8,128)} %copy-done.8, ...), custom_call_target="tpu_custom_call" | custom-call | flops 2147483648 | bytes 6291456 | tf_op jit(solution)/shard_map/pallas_call | solution.py:87
  69.3 0.0 copy-start.2
  69.3 0.0 copy-start.3
  69.3 0.0 copy-start.4
  69.3 38.7 %all_to_all.27 = bf16[16,32,1024]{2,1,0:T(8,128)(2,1)S(1)} all-to-all(bf16[16,32,1024]{2,1,0:T(8,128)(2,1)} %bitcast.24), channel_id=1, replica_groups=mesh['x'=4,'zf'=2,'zm'=2,'zp'=2,'y'=4,'zh'=2,'c'=2] {'x','zm','zp'}, dimensions={0} | all-to-all | bytes 2097152 | tf_op jit(solution)/shard_map/all_to_all | solution.py:102
  108.1 0.0 copy-done.2
  108.1 0.0 copy-done.3
  108.1 0.0 copy-done.4
  108.1 1.0 fusion.1
  109.1 18.7 %all_to_all.28 = bf16[4,32,1024]{2,1,0:T(8,128)(2,1)S(1)} all-to-all(bf16[4,32,1024]{2,1,0:T(8,128)(2,1)S(1)} %broadcast_in_dim.34), channel_id=1, replica_groups=mesh['x'=4,'zf'=2,'zm'=2,'zp'=2,'y'=4,'zh'=2,'c'=2] {'zf','zm'}, dimensions={0} | all-to-all | bytes 524288 | tf_op jit(solution)/shard_map/all_to_all | solution.py:59
  127.8 0.3 broadcast_in_dim.35
  128.1 27.1 %all_to_all.29 = bf16[8,4,32,1024]{3,2,1,0:T(8,128)(2,1)S(1)} all-to-all(bf16[8,4,32,1024]{3,2,1,0:T(8,128)(2,1)S(1)} %broadcast_in_dim.35), channel_id=1, replica_groups=mesh['x'=4,'zf'=2,'zm'=2,'zp'=2,'y'=4,'zh'=2,'c'=2] {'x','zp'}, dimensions={0} | all-to-all | bytes 4194304 | tf_op jit(solution)/shard_map/all_to_all | solution.py:59
  155.2 1.5 copy.11
  (2 shorter events, 0.0 us)
Async XLA Ops:
  0.6 59.0 %copy-start = (bf16[1024,1024]{1,0:T(8,128)(2,1)S(1)}, bf16[1024,1024]{1,0:T(8,128)(2,1)}, u32[]{:S(2)}) copy-start(bf16[1024,1024]{1,0:T(8,128)(2,1)} %param.10) | copy-start | bytes 6291460
  0.6 53.3 %copy-start.5 = (s32[512,8]{0,1:T(8,128)S(1)}, s32[512,8]{0,1:T(8,128)}, u32[]{:S(2)}) copy-start(s32[512,8]{0,1:T(8,128)} %param.8) | copy-start | bytes 49156
  0.7 53.3 %copy-start.7 = (s32[512]{0:T(512)S(1)}, s32[512]{0:T(512)}, u32[]{:S(2)}) copy-start(s32[512]{0:T(512)} %param.9) | copy-start | bytes 6148
  44.1 18.3 %copy-start.1 = (bf16[4,2,2,64,512]{4,3,2,1,0:T(8,128)(2,1)}, bf16[4,2,2,64,512]{4,3,2,1,0:T(8,128)(2,1)S(1)}, u32[]{:S(2)}) copy-start(bf16[4,2,2,64,512]{4,3,2,1,0:T(8,128)(2,1)S(1)} %all_to_all.26.own) | copy-start | bytes 3145732
  44.1 18.3 %collective-permute-start = (bf16[4,2,2,64,512]{4,3,2,1,0:T(8,128)(2,1)S(1)}, bf16[4,2,2,64,512]{4,3,2,1,0:T(8,128)(2,1)}, u32[]{:S(2)}, u32[]{:S(2)}) collective-permute-start(bf16[4,2,2,64,512]{4,3,2,1,0:T(8,128)(2,1)S(1)} %all_to_all.26.own), channel_id=1, source_target_pairs={{0,1},{1,0},{2,3},{3,2},{4,5},{5,4},{6,7},{7,6},{8,9},{9,8},{10,11... | collective-permute-start | bytes 3145736 | tf_op jit(solution)/shard_map/ppermute | solution.py:80
  54.0 8.4 %copy-start.6 = (s32[8,512]{1,0:T(8,128)}, s32[8,512]{1,0:T(8,128)S(1)}, u32[]{:S(2)}) copy-start(s32[8,512]{1,0:T(8,128)S(1)} %bitcast_select_fusion.ids_own) | copy-start | bytes 49156
  54.0 8.4 %collective-permute-start.1 = (s32[8,512]{1,0:T(8,128)S(1)}, s32[8,512]{1,0:T(8,128)S(1)}, u32[]{:S(2)}, u32[]{:S(2)}) collective-permute-start(s32[8,512]{1,0:T(8,128)S(1)} %bitcast_select_fusion.ids_own), channel_id=1, source_target_pairs={{0,64},{64,0},{1,65},{65,1},{2,66},{66,2},{3,67},{67,3},{4,68},{68... | collective-permute-start | bytes 49160 | tf_op jit(solution)/shard_map/ppermute | solution.py:76
  62.4 0.6 copy-start.8
  69.3 38.7 %copy-start.2 = (f32[32,1024]{1,0:T(8,128)S(1)}, f32[32,1024]{1,0:T(8,128)}, u32[]{:S(2)}) copy-start(f32[32,1024]{1,0:T(8,128)} %param.11) | copy-start | bytes 393220
  69.3 38.7 %copy-start.3 = (f32[32,1024]{1,0:T(8,128)S(1)}, f32[32,1024]{1,0:T(8,128)}, u32[]{:S(2)}) copy-start(f32[32,1024]{1,0:T(8,128)} %param.12) | copy-start | bytes 393220
  69.3 38.7 %copy-start.4 = (f32[32,1024]{1,0:T(8,128)S(1)}, f32[32,1024]{1,0:T(8,128)}, u32[]{:S(2)}) copy-start(f32[32,1024]{1,0:T(8,128)} %param.13) | copy-start | bytes 393220

commit v3 on v2

--- a/solution.py
+++ b/solution.py
@@ -75,14 +75,18 @@
     ids_own = jnp.where(slots < counts[None, :], positives.T, -1)
     ids_far = lax.ppermute(ids_own, "zf", SWAP)
 
-    along_z = to_all(queries.T, ("zf", "zh"))
-    along_y = to_all(along_z.reshape(zf_n, zh_n, feats, local_q), "y")
-    other = lax.ppermute(along_y, "c", SWAP)
-
     runs = weight.reshape(x_n, zf_n, near_rows, width)
     rows_w = lax.dynamic_slice_in_dim(runs, far, 1, 1)
     first = lax.axis_index(LABEL) * labels + far * near_rows
     where = jnp.stack([core, far, first]).astype(jnp.int32)
+
+    along_z = to_all(queries.T, ("zf", "zh"))
+    along_z, ids_own, ids_far, rows_w, where = lax.optimization_barrier(
+        (along_z, ids_own, ids_far, rows_w, where)
+    )
+    along_y = to_all(along_z.reshape(zf_n, zh_n, feats, local_q), "y")
+    other = lax.ppermute(along_y, "c", SWAP)
+
     vmem = pl.BlockSpec(memory_space=pltpu.VMEM)
     part = pl.pallas_call(
         grad_kernel,
@@ -98,11 +102,12 @@
         ),
     )(where, along_y, other, ids_own, ids_far, rows_w)
 
-    owners = x_n * zm_n * zp_n
-    terms = lax.all_to_all(
-        part.reshape(owners, own_rows, width), ("x", "zm", "zp"), 0, 0, tiled=True
+    by_x = lax.all_to_all(part.reshape(x_n, near_rows, width), "x", 0, 0, tiled=True)
+    by_x = summed(by_x).astype(jnp.bfloat16)
+    by_z = lax.all_to_all(
+        by_x.reshape(zm_n * zp_n, own_rows, width), ("zm", "zp"), 0, 0, tiled=True
     )
-    grad = summed(terms)
+    grad = summed(by_z)
 
     new_one = 0.9 * moment_one + 0.1 * grad
     new_two = 0.999 * moment_two + 0.001 * grad * grad

time: 158 us -> 148 us (0.937)
  blocking collectives: 127 us -> 95.6 us
  starting transfers between devices: 15.5 us -> 28.9 us
  waiting for transfers between devices: 1.05 us -> 9.25 us
    all_to_all x4 -> x3, blocking collectives: 88.1 us -> 64.1 us  [to_all(): lax.all_to_all(jnp.broadcast_to(array[None], (count, *array.shape)), axes...]
    all_to_all x0 -> x1, starting transfers between devices: none -> 15.6 us  [to_all(): lax.all_to_all(jnp.broadcast_to(array[None], (count, *array.shape)), axes...]
    all_to_all x1 -> x2, blocking collectives: 38.7 us -> 31.5 us  [the longest x1 18.4 us: per_device(): lax.all_to_all(part.reshape(x_n, near_rows, width), 'x', 0, 0, tiled=True)]
    ppermute x1, waiting for transfers between devices: 1.05 us -> 6.85 us  [per_device(): ids_far = lax.ppermute(ids_own, 'zf', SWAP)]
    ppermute x1, starting transfers between devices: 9.89 us -> 5.99 us  [per_device(): other = lax.ppermute(along_y, 'c', SWAP)]
    ppermute x1, waiting for transfers between devices: 0.01 us -> 2.4 us  [per_device(): other = lax.ppermute(along_y, 'c', SWAP)]
    ppermute x1, starting transfers between devices: 5.59 us -> 7.27 us  [per_device(): ids_far = lax.ppermute(ids_own, 'zf', SWAP)]
  transfers between devices with their start and end apart: 2 -> 3, of which waited for: 1 -> 2; matrix products, arithmetic and copies ran while one was open for 1% -> 2% of each run, Pallas kernels for 0% -> 0%
where the time goes in v3:
time: 148 us
  blocking collectives  95.6 us (65%)
  starting transfers between devices  28.9 us (20%)
  waiting for transfers between devices  9.25 us (6%)
  Pallas kernels  6.32 us (4%)
  local copies, waits for them, and re-layouts  4.65 us (3%)
  other arithmetic  2.37 us (2%)
    all_to_all x3, blocking collectives, to_all(): lax.all_to_all(jnp.broadcast_to(array[None], (count, *array.shape)), axes...  64.1 us
    all_to_all x1, blocking collectives, per_device(): lax.all_to_all(part.reshape(x_n, near_rows, width), 'x', 0, 0, tiled=True)  18.4 us
    all_to_all x1, starting transfers between devices, to_all(): lax.all_to_all(jnp.broadcast_to(array[None], (count, *array.shape)), axes...  15.6 us
    all_to_all x1, blocking collectives, per_device(): lax.all_to_all(by_x.reshape(zm_n * zp_n, own_rows, width), ('zm', 'zp'),...  13.1 us
    ppermute x1, starting transfers between devices, per_device(): ids_far = lax.ppermute(ids_own, 'zf', SWAP)  7.27 us
    ppermute x1, waiting for transfers between devices, per_device(): ids_far = lax.ppermute(ids_own, 'zf', SWAP)  6.85 us
    pallas_call x1, Pallas kernels, per_device(): pl.pallas_call(grad_kernel, out_shape=jax.ShapeDtypeStruct((rows, width),...  6.32 us
    ppermute x1, starting transfers between devices, per_device(): other = lax.ppermute(along_y, 'c', SWAP)  5.99 us
  transfers between devices with their start and end apart: 3, of which 2 were waited for; matrix products, arithmetic and copies ran while one was open for 2% of the time, Pallas kernels for 0%

profile of v3, /device:TPU:1, one launch (start us, length us, event | category | flops | bytes accessed | tf_op | source)
XLA Modules:
  0.0 147.8 jit_solution(10966519743484138023)
XLA Ops:
  0.6 0.0 copy-start
  0.6 1.7 %broadcast_in_dim.14 = bf16[4,64,512]{2,1,0:T(8,128)(2,1)} broadcast(bf16[64,512]{1,0:T(8,128)(2,1)} %bitcast.27), dimensions={1,2} | broadcast | bytes 327680 | tf_op jit(solution)/shard_map/broadcast_in_dim | solution.py:60
  2.4 15.6 %all-to-all-start = ((bf16[4,64,512]{2,1,0:T(8,128)(2,1)}), bf16[4,64,512]{2,1,0:T(8,128)(2,1)S(1)}, u32[]{:S(2)}, u32[]{:S(2)}) async-start(bf16[4,64,512]{2,1,0:T(8,128)(2,1)} %broadcast_in_dim.14), calls=%async_computation | async-start | bytes 524288 | tf_op jit(solution)/shard_map/all_to_all | solution.py:59
  18.0 0.7 bitcast_select_fusion.ids_own
  18.7 0.0 copy-start.5
  18.7 7.3 %collective-permute-start = (s32[8,512]{1,0:T(8,128)S(1)}, s32[8,512]{1,0:T(8,128)S(1)}, u32[]{:S(2)}, u32[]{:S(2)}) collective-permute-start(s32[8,512]{1,0:T(8,128)S(1)} %bitcast_select_fusion.ids_own), channel_id=1, source_target_pairs={{0,64},{64,0},{1,65},{65,1},{2,66},{66,2},{3,67},{67,3},{4,68},{68... | collective-permute-start | bytes 49160 | tf_op jit(solution)/shard_map/ppermute | solution.py:76
  26.0 0.0 copy-done
  26.0 1.0 constant_dynamic-slice_fusion.weight
  27.0 0.7 pad_add_fusion.where
  27.7 6.9 %collective-permute-done.ids_far = s32[8,512]{1,0:T(8,128)S(1)} collective-permute-done((s32[8,512]{1,0:T(8,128)S(1)}, s32[8,512]{1,0:T(8,128)S(1)}, u32[]{:S(2)}, u32[]{:S(2)}) %collective-permute-start) | collective-permute-done | bytes 16416 | tf_op jit(solution)/shard_map/ppermute | solution.py:76
  34.5 0.0 copy-start.6
  34.6 0.0 all-to-all-done
  34.6 0.1 broadcast_in_dim.17
  34.7 15.9 %all_to_all.30.own = bf16[4,2,2,64,512]{4,3,2,1,0:T(8,128)(2,1)S(1)} all-to-all(bf16[4,2,2,64,512]{4,3,2,1,0:T(8,128)(2,1)S(1)} %broadcast_in_dim.17), channel_id=1, replica_groups=mesh['x'=4,'zf'=2,'zm'=2,'zp'=2,'y'=4,'zh'=2,'c'=2] {'y'}, dimensions={0} | all-to-all | bytes 2097152 | tf_op jit(solution)/shard_map/all_to_all | solution.py:59
  50.6 0.0 copy-done.5
  50.6 0.0 copy-start.1
  50.6 6.0 %collective-permute-start.1 = (bf16[4,2,2,64,512]{4,3,2,1,0:T(8,128)(2,1)S(1)}, bf16[4,2,2,64,512]{4,3,2,1,0:T(8,128)(2,1)}, u32[]{:S(2)}, u32[]{:S(2)}) collective-permute-start(bf16[4,2,2,64,512]{4,3,2,1,0:T(8,128)(2,1)S(1)} %all_to_all.30.own), channel_id=1, source_target_pairs={{0,1},{1,0},{2,3},{3,2},{4,5},{5,4},{6,7},{7,6},{8,9},{9,8},{10,11... | collective-permute-start | bytes 3145736 | tf_op jit(solution)/shard_map/ppermute | solution.py:88
  56.6 2.4 %collective-permute-done.1.other = bf16[4,2,2,64,512]{4,3,2,1,0:T(8,128)(2,1)} collective-permute-done((bf16[4,2,2,64,512]{4,3,2,1,0:T(8,128)(2,1)S(1)}, bf16[4,2,2,64,512]{4,3,2,1,0:T(8,128)(2,1)}, u32[]{:S(2)}, u32[]{:S(2)}) %collective-permute-start.1) | collective-permute-done | bytes 1048608 | tf_op jit(solution)/shard_map/ppermute | solution.py:88
  59.0 0.0 copy-done.6
  59.0 0.0 copy-done.1
  59.0 6.3 %shard_map.102 = bf16[512,1024]{1,0:T(8,128)(2,1)} custom-call(s32[3]{0:T(128)} %pad_add_fusion.where, bf16[4,2,2,64,512]{4,3,2,1,0:T(8,128)(2,1)} %copy-done.1, bf16[4,2,2,64,512]{4,3,2,1,0:T(8,128)(2,1)} %collective-permute-done.1.other, s32[8,512]{1,0:T(8,128)} %copy-done.5, s32[8,512]{1,0:T(8,128)} %copy-done.6, ...), custom_call_target="tpu_custom_call" | custom-call | flops 2147483648 | bytes 6291456 | tf_op jit(solution)/shard_map/pallas_call | solution.py:91
  65.3 0.0 copy-start.2
  65.3 0.0 copy-start.3
  65.3 0.0 copy-start.4
  65.3 18.4 %all_to_all.31 = bf16[4,128,1024]{2,1,0:T(8,128)(2,1)S(1)} all-to-all(bf16[4,128,1024]{2,1,0:T(8,128)(2,1)} %bitcast.26), channel_id=1, replica_groups=mesh['x'=4,'zf'=2,'zm'=2,'zp'=2,'y'=4,'zh'=2,'c'=2] {'x'}, dimensions={0} | all-to-all | bytes 2097152 | tf_op jit(solution)/shard_map/all_to_all | solution.py:105
  83.7 0.2 add_convert_fusion
  83.9 13.1 %all_to_all.32 = bf16[4,32,1024]{2,1,0:T(8,128)(2,1)S(1)} all-to-all(bf16[4,32,1024]{2,1,0:T(8,128)(2,1)S(1)} %bitcast.25), channel_id=1, replica_groups=mesh['x'=4,'zf'=2,'zm'=2,'zp'=2,'y'=4,'zh'=2,'c'=2] {'zm','zp'}, dimensions={0} | all-to-all | bytes 524288 | tf_op jit(solution)/shard_map/all_to_all | solution.py:107
  97.0 0.0 copy-done.2
  97.0 0.0 copy-done.3
  97.0 0.0 copy-done.4
  97.0 0.8 fusion.2
  97.9 12.2 %all_to_all.33 = bf16[4,32,1024]{2,1,0:T(8,128)(2,1)S(1)} all-to-all(bf16[4,32,1024]{2,1,0:T(8,128)(2,1)S(1)} %broadcast_in_dim.34), channel_id=1, replica_groups=mesh['x'=4,'zf'=2,'zm'=2,'zp'=2,'y'=4,'zh'=2,'c'=2] {'zf','zm'}, dimensions={0} | all-to-all | bytes 524288 | tf_op jit(solution)/shard_map/all_to_all | solution.py:59
  110.1 0.3 broadcast_in_dim.35
  110.4 35.9 %all_to_all.34 = bf16[8,4,32,1024]{3,2,1,0:T(8,128)(2,1)S(1)} all-to-all(bf16[8,4,32,1024]{3,2,1,0:T(8,128)(2,1)S(1)} %broadcast_in_dim.35), channel_id=1, replica_groups=mesh['x'=4,'zf'=2,'zm'=2,'zp'=2,'y'=4,'zh'=2,'c'=2] {'x','zp'}, dimensions={0} | all-to-all | bytes 4194304 | tf_op jit(solution)/shard_map/all_to_all | solution.py:59
  146.3 1.5 %copy.11 = bf16[4,4,2,32,1024]{4,3,2,1,0:T(8,128)(2,1)} copy(bf16[4,4,2,32,1024]{4,3,1,2,0:T(8,128)(2,1)S(1)} %bitcast.22) | data formatting | bytes 4194304 | tf_op jit(solution)/shard_map/transpose | solution.py:121
  (1 shorter events, 0.0 us)
Async XLA Ops:
  0.6 25.4 %copy-start = (bf16[1024,1024]{1,0:T(8,128)(2,1)S(1)}, bf16[1024,1024]{1,0:T(8,128)(2,1)}, u32[]{:S(2)}) copy-start(bf16[1024,1024]{1,0:T(8,128)(2,1)} %param.10) | copy-start | bytes 6291460
  2.4 32.2 %all-to-all-start = ((bf16[4,64,512]{2,1,0:T(8,128)(2,1)}), bf16[4,64,512]{2,1,0:T(8,128)(2,1)S(1)}, u32[]{:S(2)}, u32[]{:S(2)}) async-start(bf16[4,64,512]{2,1,0:T(8,128)(2,1)} %broadcast_in_dim.14), calls=%async_computation | async-start | bytes 524288 | tf_op jit(solution)/shard_map/all_to_all | solution.py:59
  18.7 31.9 %copy-start.5 = (s32[8,512]{1,0:T(8,128)}, s32[8,512]{1,0:T(8,128)S(1)}, u32[]{:S(2)}) copy-start(s32[8,512]{1,0:T(8,128)S(1)} %bitcast_select_fusion.ids_own) | copy-start | bytes 49156
  18.7 15.8 %collective-permute-start = (s32[8,512]{1,0:T(8,128)S(1)}, s32[8,512]{1,0:T(8,128)S(1)}, u32[]{:S(2)}, u32[]{:S(2)}) collective-permute-start(s32[8,512]{1,0:T(8,128)S(1)} %bitcast_select_fusion.ids_own), channel_id=1, source_target_pairs={{0,64},{64,0},{1,65},{65,1},{2,66},{66,2},{3,67},{67,3},{4,68},{68... | collective-permute-start | bytes 49160 | tf_op jit(solution)/shard_map/ppermute | solution.py:76
  34.5 24.5 %copy-start.6 = (s32[8,512]{1,0:T(8,128)}, s32[8,512]{1,0:T(8,128)S(1)}, u32[]{:S(2)}) copy-start(s32[8,512]{1,0:T(8,128)S(1)} %collective-permute-done.ids_far) | copy-start | bytes 49156
  50.6 8.4 %copy-start.1 = (bf16[4,2,2,64,512]{4,3,2,1,0:T(8,128)(2,1)}, bf16[4,2,2,64,512]{4,3,2,1,0:T(8,128)(2,1)S(1)}, u32[]{:S(2)}) copy-start(bf16[4,2,2,64,512]{4,3,2,1,0:T(8,128)(2,1)S(1)} %all_to_all.30.own) | copy-start | bytes 3145732
  50.6 8.4 %collective-permute-start.1 = (bf16[4,2,2,64,512]{4,3,2,1,0:T(8,128)(2,1)S(1)}, bf16[4,2,2,64,512]{4,3,2,1,0:T(8,128)(2,1)}, u32[]{:S(2)}, u32[]{:S(2)}) collective-permute-start(bf16[4,2,2,64,512]{4,3,2,1,0:T(8,128)(2,1)S(1)} %all_to_all.30.own), channel_id=1, source_target_pairs={{0,1},{1,0},{2,3},{3,2},{4,5},{5,4},{6,7},{7,6},{8,9},{9,8},{10,11... | collective-permute-start | bytes 3145736 | tf_op jit(solution)/shard_map/ppermute | solution.py:88
  65.3 31.7 %copy-start.2 = (f32[32,1024]{1,0:T(8,128)S(1)}, f32[32,1024]{1,0:T(8,128)}, u32[]{:S(2)}) copy-start(f32[32,1024]{1,0:T(8,128)} %param.11) | copy-start | bytes 393220
  65.3 31.7 %copy-start.3 = (f32[32,1024]{1,0:T(8,128)S(1)}, f32[32,1024]{1,0:T(8,128)}, u32[]{:S(2)}) copy-start(f32[32,1024]{1,0:T(8,128)} %param.12) | copy-start | bytes 393220
  65.3 31.7 %copy-start.4 = (f32[32,1024]{1,0:T(8,128)S(1)}, f32[32,1024]{1,0:T(8,128)}, u32[]{:S(2)}) copy-start(f32[32,1024]{1,0:T(8,128)} %param.13) | copy-start | bytes 393220

commit v4 on v3

--- a/solution.py
+++ b/solution.py
@@ -11,33 +11,48 @@
 DP = ("x", "zf", "zm", "zp")
 LABEL = ("y", "zh", "c")
 SWAP = [(0, 1), (1, 0)]
+STAGGER_NS = 10000
 
 
-def grad_kernel(where, own, other, ids_own, ids_far, weight, out, whole, ids):
-    core, far, first_label = where[0], where[1], where[2]
+def grad_kernel(own, other, ids, weight, out, whole, rows_w, w_sems, own_sems, other_sems):
+    core, far = lax.axis_index("c"), lax.axis_index("zf")
+    label_block = lax.axis_index("y") * 4 + lax.axis_index("zh") * 2 + core
     ys, blocks, halves, feats = own.shape[:4]
     runs, _, run_rows, width = weight.shape
     rows = runs * run_rows
-    for y in range(ys):
-        for block in range(blocks):
+    fetched = []
+    for run in range(runs):
+        fetched.append(pltpu.make_async_copy(
+            weight.at[run, far], rows_w.at[pl.ds(run * run_rows, run_rows)], w_sems.at[run]))
+        fetched[-1].start()
+    placed = []
+    for block in range(blocks):
+        placed.append([])
+        for y in range(ys):
             for half in range(halves):
                 at = (y * halves + half) * 2 * feats
-                mine = pl.ds(pl.multiple_of(at + core * feats, feats), feats)
-                theirs = pl.ds(pl.multiple_of(at + (1 - core) * feats, feats), feats)
-                whole[block, mine, :] = own[y, block, half]
-                whole[block, theirs, :] = other[y, block, half]
-    ids[pl.ds(far, 1)] = ids_own[...][None]
-    ids[pl.ds(1 - far, 1)] = ids_far[...][None]
-    rows_w = weight[...].reshape(rows, width)
+                for src, sems, which in ((own, own_sems, core), (other, other_sems, 1 - core)):
+                    rows_at = pl.ds(pl.multiple_of(at + which * feats, feats), feats)
+                    placed[block].append(pltpu.make_async_copy(
+                        src.at[y, block, half], whole.at[block, rows_at],
+                        sems.at[(block * ys + y) * halves + half]))
+                    placed[block][-1].start()
     row = lax.broadcasted_iota(jnp.int32, (rows, 1), 0)
+    first_label = label_block * (2 * rows) + far * run_rows
     label = first_label + (row // run_rows) * (2 * run_rows) + row % run_rows
+    for copy in fetched:
+        copy.wait()
     total = None
     for block in range(blocks):
+        high, low = ids[block, 0].astype(jnp.float32), ids[block, 1].astype(jnp.float32)
+        slots = (high * 128.0 + low).astype(jnp.int32)
+        for copy in placed[block]:
+            copy.wait()
         block_q = whole[block]
-        logits = jnp.dot(rows_w, block_q, preferred_element_type=jnp.float32)
-        hit = label == ids[block, 0:1, :]
-        for slot in range(1, ids.shape[1]):
-            hit = hit | (label == ids[block, slot : slot + 1, :])
+        logits = jnp.dot(rows_w[...], block_q, preferred_element_type=jnp.float32)
+        hit = label == slots[0:1, :]
+        for slot in range(1, slots.shape[0]):
+            hit = hit | (label == slots[slot : slot + 1, :])
         diff = jax.nn.sigmoid(logits) - hit.astype(jnp.float32)
         grad_logit = (diff * (1.0 / 16384)).astype(jnp.bfloat16)
         part = lax.dot_general(
@@ -45,6 +60,10 @@
         )
         total = part if total is None else total + part
     out[...] = total.astype(jnp.bfloat16)
+    if STAGGER_NS:
+        @pl.when(core == 1)
+        def _():
+            pl.delay(STAGGER_NS)
 
 
 def summed(terms):
@@ -67,40 +86,38 @@
     own_rows = master.shape[0]
     x_n, zf_n, zm_n, zp_n = (lax.axis_size(a) for a in DP)
     y_n, zh_n, c_n = (lax.axis_size(a) for a in LABEL)
-    core, far = lax.axis_index("c"), lax.axis_index("zf")
     near_rows = zm_n * zp_n * own_rows
     rows = x_n * near_rows
 
     slots = lax.broadcasted_iota(jnp.int32, (positives.shape[1], local_q), 0)
-    ids_own = jnp.where(slots < counts[None, :], positives.T, -1)
-    ids_far = lax.ppermute(ids_own, "zf", SWAP)
+    ids = jnp.where(slots < counts[None, :], positives.T, -1)
+    ids = jnp.where(lax.axis_index("zh") == 0, ids >> 7, ids & 127).astype(jnp.bfloat16)
 
-    runs = weight.reshape(x_n, zf_n, near_rows, width)
-    rows_w = lax.dynamic_slice_in_dim(runs, far, 1, 1)
-    first = lax.axis_index(LABEL) * labels + far * near_rows
-    where = jnp.stack([core, far, first]).astype(jnp.int32)
-
-    along_z = to_all(queries.T, ("zf", "zh"))
-    along_z, ids_own, ids_far, rows_w, where = lax.optimization_barrier(
-        (along_z, ids_own, ids_far, rows_w, where)
-    )
-    along_y = to_all(along_z.reshape(zf_n, zh_n, feats, local_q), "y")
+    along_z = to_all(jnp.concatenate([queries.T, ids]), ("zf", "zh"))
+    along_z = along_z.reshape(zf_n, zh_n, feats + ids.shape[0], local_q)
+    along_y = to_all(along_z[:, :, :feats], "y")
     other = lax.ppermute(along_y, "c", SWAP)
 
     vmem = pl.BlockSpec(memory_space=pltpu.VMEM)
+    anywhere = pl.BlockSpec(memory_space=pl.ANY)
+    pieces = zf_n * y_n * zh_n
     part = pl.pallas_call(
         grad_kernel,
         out_shape=jax.ShapeDtypeStruct((rows, width), jnp.bfloat16),
-        in_specs=[pl.BlockSpec(memory_space=pltpu.SMEM)] + [vmem] * 5,
+        in_specs=[anywhere, anywhere, vmem, anywhere],
         out_specs=vmem,
         scratch_shapes=[
             pltpu.VMEM((zf_n, width, local_q), jnp.bfloat16),
-            pltpu.VMEM((zf_n, positives.shape[1], local_q), jnp.int32),
+            pltpu.VMEM((rows, width), jnp.bfloat16),
+            pltpu.SemaphoreType.DMA((x_n,)),
+            pltpu.SemaphoreType.DMA((pieces,)),
+            pltpu.SemaphoreType.DMA((pieces,)),
         ],
+        compiler_params=pltpu.CompilerParams(vmem_limit_bytes=32 << 20),
         cost_estimate=pl.CostEstimate(
             flops=4 * rows * width * zf_n * local_q, bytes_accessed=6 << 20, transcendentals=0
         ),
-    )(where, along_y, other, ids_own, ids_far, rows_w)
+    )(along_y, other, along_z[:, :, feats:], weight.reshape(x_n, zf_n, near_rows, width))
 
     by_x = lax.all_to_all(part.reshape(x_n, near_rows, width), "x", 0, 0, tiled=True)
     by_x = summed(by_x).astype(jnp.bfloat16)

time: 148 us -> 146 us (0.986)
  starting transfers between devices: 28.9 us -> 8.98 us
  blocking collectives: 95.6 us -> 112 us
  Pallas kernels: 6.32 us -> 17.2 us
  waiting for transfers between devices: 9.25 us -> 2.25 us
  local copies, waits for them, and re-layouts: 4.65 us -> 1.92 us
    all_to_all x3 -> x4, blocking collectives: 64.1 us -> 82.8 us  [to_all(): lax.all_to_all(jnp.broadcast_to(array[None], (count, *array.shape)), axes...]
    all_to_all x1 -> x0, starting transfers between devices: 15.6 us -> none  [to_all(): lax.all_to_all(jnp.broadcast_to(array[None], (count, *array.shape)), axes...]
    pallas_call x1, Pallas kernels: 6.32 us -> 17.2 us  [per_device(): pl.pallas_call(grad_kernel, out_shape=jax.ShapeDtypeStruct((rows, width),...]
    ppermute x1 -> x0, starting transfers between devices: 7.27 us -> none  [per_device(): ids_far = lax.ppermute(ids_own, 'zf', SWAP)]
    ppermute x1 -> x0, waiting for transfers between devices: 6.85 us -> none  [per_device(): ids_far = lax.ppermute(ids_own, 'zf', SWAP)]
    all_to_all x1, blocking collectives: 18.4 us -> 13.7 us  [per_device(): lax.all_to_all(part.reshape(x_n, near_rows, width), 'x', 0, 0, tiled=True)]
    ppermute x1, starting transfers between devices: 5.99 us -> 8.98 us  [per_device(): other = lax.ppermute(along_y, 'c', SWAP)]
    all_to_all x1, blocking collectives: 13.1 us -> 15.7 us  [per_device(): lax.all_to_all(by_x.reshape(zm_n * zp_n, own_rows, width), ('zm', 'zp'),...]
  transfers between devices with their start and end apart: 3 -> 1, of which waited for: 2 -> 1; matrix products, arithmetic and copies ran while one was open for 2% -> 0% of each run, Pallas kernels for 0% -> 0%
where the time goes in v4:
time: 146 us
  blocking collectives  112 us (77%)
  Pallas kernels  17.2 us (12%)
  starting transfers between devices  8.98 us (6%)
  other arithmetic  2.57 us (2%)
  waiting for transfers between devices  2.25 us (2%)
  local copies, waits for them, and re-layouts  1.92 us (1%)
    all_to_all x4, blocking collectives, to_all(): lax.all_to_all(jnp.broadcast_to(array[None], (count, *array.shape)), axes...  82.8 us
    pallas_call x1, Pallas kernels, per_device(): pl.pallas_call(grad_kernel, out_shape=jax.ShapeDtypeStruct((rows, width),...  17.2 us
    all_to_all x1, blocking collectives, per_device(): lax.all_to_all(by_x.reshape(zm_n * zp_n, own_rows, width), ('zm', 'zp'),...  15.7 us
    all_to_all x1, blocking collectives, per_device(): lax.all_to_all(part.reshape(x_n, near_rows, width), 'x', 0, 0, tiled=True)  13.7 us
    ppermute x1, starting transfers between devices, per_device(): other = lax.ppermute(along_y, 'c', SWAP)  8.98 us
  transfers between devices with their start and end apart: 1, of which 1 were waited for; matrix products, arithmetic and copies ran while one was open for 0% of the time, Pallas kernels for 0%

profile of v4, /device:TPU:1, one launch (start us, length us, event | category | flops | bytes accessed | tf_op | source)
XLA Modules:
  0.0 145.8 jit_solution(8189791699440947351)
XLA Ops:
  0.6 0.7 select_convert_fusion
  1.4 0.8 pad_maximum_fusion
  2.2 30.1 %all_to_all.30 = bf16[4,72,512]{2,1,0:T(8,128)(2,1)S(1)} all-to-all(bf16[4,72,512]{2,1,0:T(8,128)(2,1)S(1)} %broadcast_in_dim.13), channel_id=1, replica_groups=mesh['x'=4,'zf'=2,'zm'=2,'zp'=2,'y'=4,'zh'=2,'c'=2] {'zf','zh'}, dimensions={0} | all-to-all | bytes 589824 | tf_op jit(solution)/shard_map/all_to_all | solution.py:78
  32.3 0.0 copy-start
  32.3 0.1 broadcast_in_dim.14
  32.4 13.9 %all_to_all.31.own = bf16[4,2,2,64,512]{4,3,2,1,0:T(8,128)(2,1)S(1)} all-to-all(bf16[4,2,2,64,512]{4,3,2,1,0:T(8,128)(2,1)S(1)} %broadcast_in_dim.14), channel_id=1, replica_groups=mesh['x'=4,'zf'=2,'zm'=2,'zp'=2,'y'=4,'zh'=2,'c'=2] {'y'}, dimensions={0} | all-to-all | bytes 2097152 | tf_op jit(solution)/shard_map/all_to_all | solution.py:78
  46.3 9.0 %collective-permute-start = (bf16[4,2,2,64,512]{4,3,2,1,0:T(8,128)(2,1)S(1)}, bf16[4,2,2,64,512]{4,3,2,1,0:T(8,128)(2,1)S(1)}, u32[]{:S(2)}, u32[]{:S(2)}) collective-permute-start(bf16[4,2,2,64,512]{4,3,2,1,0:T(8,128)(2,1)S(1)} %all_to_all.31.own), channel_id=1, source_target_pairs={{0,1},{1,0},{2,3},{3,2},{4,5},{5,4},{6,7},{7,6},{8,9},{9,8},{10,11... | collective-permute-start | bytes 3145736 | tf_op jit(solution)/shard_map/ppermute | solution.py:99
  55.3 2.3 %collective-permute-done.other = bf16[4,2,2,64,512]{4,3,2,1,0:T(8,128)(2,1)S(1)} collective-permute-done((bf16[4,2,2,64,512]{4,3,2,1,0:T(8,128)(2,1)S(1)}, bf16[4,2,2,64,512]{4,3,2,1,0:T(8,128)(2,1)S(1)}, u32[]{:S(2)}, u32[]{:S(2)}) %collective-permute-start) | collective-permute-done | bytes 1048608 | tf_op jit(solution)/shard_map/ppermute | solution.py:99
  57.6 0.0 copy-done
  57.6 17.2 %shard_map.102 = bf16[512,1024]{1,0:T(8,128)(2,1)S(1)} custom-call(bf16[4,2,2,64,512]{4,3,2,1,0:T(8,128)(2,1)S(1)} %all_to_all.31.own, bf16[4,2,2,64,512]{4,3,2,1,0:T(8,128)(2,1)S(1)} %collective-permute-done.other, bf16[2,2,8,512]{3,2,1,0:T(8,128)(2,1)S(1)} %slice.41.ids, bf16[4,2,128,1024]{3,2,1,0:T(8,128)(2,1)S(1)} %bitcast.21), custom_call_target="tpu_custom_call" | custom-call | flops 2147483648 | bytes 6291456 | tf_op jit(solution)/shard_map/pallas_call | solution.py:104
  74.7 0.0 copy-start.1
  74.8 0.0 copy-start.2
  74.8 0.0 copy-start.3
  74.8 13.7 %all_to_all.32 = bf16[4,128,1024]{2,1,0:T(8,128)(2,1)S(1)} all-to-all(bf16[4,128,1024]{2,1,0:T(8,128)(2,1)S(1)} %bitcast.20), channel_id=1, replica_groups=mesh['x'=4,'zf'=2,'zm'=2,'zp'=2,'y'=4,'zh'=2,'c'=2] {'x'}, dimensions={0} | all-to-all | bytes 2097152 | tf_op jit(solution)/shard_map/all_to_all | solution.py:122
  88.5 0.2 add_convert_fusion
  88.7 15.7 %all_to_all.33 = bf16[4,32,1024]{2,1,0:T(8,128)(2,1)S(1)} all-to-all(bf16[4,32,1024]{2,1,0:T(8,128)(2,1)S(1)} %bitcast.26), channel_id=1, replica_groups=mesh['x'=4,'zf'=2,'zm'=2,'zp'=2,'y'=4,'zh'=2,'c'=2] {'zm','zp'}, dimensions={0} | all-to-all | bytes 524288 | tf_op jit(solution)/shard_map/all_to_all | solution.py:124
  104.3 0.0 copy-done.1
  104.3 0.0 copy-done.2
  104.3 0.0 copy-done.3
  104.4 0.8 fusion.2
  105.2 13.7 %all_to_all.34 = bf16[4,32,1024]{2,1,0:T(8,128)(2,1)S(1)} all-to-all(bf16[4,32,1024]{2,1,0:T(8,128)(2,1)S(1)} %broadcast_in_dim.15), channel_id=1, replica_groups=mesh['x'=4,'zf'=2,'zm'=2,'zp'=2,'y'=4,'zh'=2,'c'=2] {'zf','zm'}, dimensions={0} | all-to-all | bytes 524288 | tf_op jit(solution)/shard_map/all_to_all | solution.py:78
  118.9 0.3 broadcast_in_dim.16
  119.2 25.2 %all_to_all.35 = bf16[8,4,32,1024]{3,2,1,0:T(8,128)(2,1)S(1)} all-to-all(bf16[8,4,32,1024]{3,2,1,0:T(8,128)(2,1)S(1)} %broadcast_in_dim.16), channel_id=1, replica_groups=mesh['x'=4,'zf'=2,'zm'=2,'zp'=2,'y'=4,'zh'=2,'c'=2] {'x','zp'}, dimensions={0} | all-to-all | bytes 4194304 | tf_op jit(solution)/shard_map/all_to_all | solution.py:78
  144.3 1.5 %copy.11 = bf16[4,4,2,32,1024]{4,3,2,1,0:T(8,128)(2,1)} copy(bf16[4,4,2,32,1024]{4,3,1,2,0:T(8,128)(2,1)S(1)} %bitcast.22) | data formatting | bytes 4194304 | tf_op jit(solution)/shard_map/transpose | solution.py:138
  (4 shorter events, 0.1 us)
Async XLA Ops:
  32.3 25.2 %copy-start = (bf16[1024,1024]{1,0:T(8,128)(2,1)S(1)}, bf16[1024,1024]{1,0:T(8,128)(2,1)}, u32[]{:S(2)}) copy-start(bf16[1024,1024]{1,0:T(8,128)(2,1)} %param.10) | copy-start | bytes 6291460
  46.3 11.3 %collective-permute-start = (bf16[4,2,2,64,512]{4,3,2,1,0:T(8,128)(2,1)S(1)}, bf16[4,2,2,64,512]{4,3,2,1,0:T(8,128)(2,1)S(1)}, u32[]{:S(2)}, u32[]{:S(2)}) collective-permute-start(bf16[4,2,2,64,512]{4,3,2,1,0:T(8,128)(2,1)S(1)} %all_to_all.31.own), channel_id=1, source_target_pairs={{0,1},{1,0},{2,3},{3,2},{4,5},{5,4},{6,7},{7,6},{8,9},{9,8},{10,11... | collective-permute-start | bytes 3145736 | tf_op jit(solution)/shard_map/ppermute | solution.py:99
  74.7 29.6 %copy-start.1 = (f32[32,1024]{1,0:T(8,128)S(1)}, f32[32,1024]{1,0:T(8,128)}, u32[]{:S(2)}) copy-start(f32[32,1024]{1,0:T(8,128)} %param.11) | copy-start | bytes 393220
  74.8 29.6 %copy-start.2 = (f32[32,1024]{1,0:T(8,128)S(1)}, f32[32,1024]{1,0:T(8,128)}, u32[]{:S(2)}) copy-start(f32[32,1024]{1,0:T(8,128)} %param.12) | copy-start | bytes 393220
  74.8 29.6 %copy-start.3 = (f32[32,1024]{1,0:T(8,128)S(1)}, f32[32,1024]{1,0:T(8,128)}, u32[]{:S(2)}) copy-start(f32[32,1024]{1,0:T(8,128)} %param.13) | copy-start | bytes 393220

commit v5 on v4

--- a/solution.py
+++ b/solution.py
@@ -11,10 +11,10 @@
 DP = ("x", "zf", "zm", "zp")
 LABEL = ("y", "zh", "c")
 SWAP = [(0, 1), (1, 0)]
-STAGGER_NS = 10000
+STAGGER_NS = 8000
 
 
-def grad_kernel(own, other, ids, weight, out, whole, rows_w, w_sems, own_sems, other_sems):
+def grad_kernel(own, other, ids, weight, out, whole, rows_w, w_sems):
     core, far = lax.axis_index("c"), lax.axis_index("zf")
     label_block = lax.axis_index("y") * 4 + lax.axis_index("zh") * 2 + core
     ys, blocks, halves, feats = own.shape[:4]
@@ -25,18 +25,14 @@
         fetched.append(pltpu.make_async_copy(
             weight.at[run, far], rows_w.at[pl.ds(run * run_rows, run_rows)], w_sems.at[run]))
         fetched[-1].start()
-    placed = []
-    for block in range(blocks):
-        placed.append([])
-        for y in range(ys):
+    for y in range(ys):
+        for block in range(blocks):
             for half in range(halves):
                 at = (y * halves + half) * 2 * feats
-                for src, sems, which in ((own, own_sems, core), (other, other_sems, 1 - core)):
-                    rows_at = pl.ds(pl.multiple_of(at + which * feats, feats), feats)
-                    placed[block].append(pltpu.make_async_copy(
-                        src.at[y, block, half], whole.at[block, rows_at],
-                        sems.at[(block * ys + y) * halves + half]))
-                    placed[block][-1].start()
+                mine = pl.ds(pl.multiple_of(at + core * feats, feats), feats)
+                theirs = pl.ds(pl.multiple_of(at + (1 - core) * feats, feats), feats)
+                whole[block, mine, :] = own[y, block, half]
+                whole[block, theirs, :] = other[y, block, half]
     row = lax.broadcasted_iota(jnp.int32, (rows, 1), 0)
     first_label = label_block * (2 * rows) + far * run_rows
     label = first_label + (row // run_rows) * (2 * run_rows) + row % run_rows
@@ -46,8 +42,6 @@
     for block in range(blocks):
         high, low = ids[block, 0].astype(jnp.float32), ids[block, 1].astype(jnp.float32)
         slots = (high * 128.0 + low).astype(jnp.int32)
-        for copy in placed[block]:
-            copy.wait()
         block_q = whole[block]
         logits = jnp.dot(rows_w[...], block_q, preferred_element_type=jnp.float32)
         hit = label == slots[0:1, :]
@@ -59,7 +53,13 @@
             grad_logit, block_q, (((1,), (1,)), ((), ())), preferred_element_type=jnp.float32
         )
         total = part if total is None else total + part
-    out[...] = total.astype(jnp.bfloat16)
+    xs, zs, own_rows = out.shape[0], out.shape[1], out.shape[2]
+    for x in range(xs):
+        for z in range(zs):
+            at = (x * zs + z) * own_rows
+            out[jnp.where(core == 0, x, z), jnp.where(core == 0, z, x)] = total[
+                at : at + own_rows
+            ].astype(jnp.bfloat16)
     if STAGGER_NS:
         @pl.when(core == 1)
         def _():
@@ -100,18 +100,16 @@
 
     vmem = pl.BlockSpec(memory_space=pltpu.VMEM)
     anywhere = pl.BlockSpec(memory_space=pl.ANY)
-    pieces = zf_n * y_n * zh_n
+    zs = zm_n * zp_n
     part = pl.pallas_call(
         grad_kernel,
-        out_shape=jax.ShapeDtypeStruct((rows, width), jnp.bfloat16),
-        in_specs=[anywhere, anywhere, vmem, anywhere],
+        out_shape=jax.ShapeDtypeStruct((x_n, zs, own_rows, width), jnp.bfloat16),
+        in_specs=[vmem, vmem, vmem, anywhere],
         out_specs=vmem,
         scratch_shapes=[
             pltpu.VMEM((zf_n, width, local_q), jnp.bfloat16),
             pltpu.VMEM((rows, width), jnp.bfloat16),
             pltpu.SemaphoreType.DMA((x_n,)),
-            pltpu.SemaphoreType.DMA((pieces,)),
-            pltpu.SemaphoreType.DMA((pieces,)),
         ],
         compiler_params=pltpu.CompilerParams(vmem_limit_bytes=32 << 20),
         cost_estimate=pl.CostEstimate(
@@ -119,12 +117,20 @@
         ),
     )(along_y, other, along_z[:, :, feats:], weight.reshape(x_n, zf_n, near_rows, width))
 
-    by_x = lax.all_to_all(part.reshape(x_n, near_rows, width), "x", 0, 0, tiled=True)
-    by_x = summed(by_x).astype(jnp.bfloat16)
-    by_z = lax.all_to_all(
-        by_x.reshape(zm_n * zp_n, own_rows, width), ("zm", "zp"), 0, 0, tiled=True
+    def member(x, z, core):
+        return (x * zs + z) * c_n + core
+
+    over_x = [[[member(x, z, core) for x in range(x_n)] for z in range(zs)] for core in range(c_n)]
+    over_z = [[[member(x, z, core) for z in range(zs)] for x in range(x_n)] for core in range(c_n)]
+    axes = ("x", "zm", "zp", "c")
+    terms = lax.all_to_all(
+        part, axes, 0, 0, axis_index_groups=over_x[0] + over_z[1], tiled=True
     )
-    grad = summed(by_z)
+    terms = summed(terms).astype(jnp.bfloat16)
+    terms = lax.all_to_all(
+        terms, axes, 0, 0, axis_index_groups=over_z[0] + over_x[1], tiled=True
+    )
+    grad = summed(terms)
 
     new_one = 0.9 * moment_one + 0.1 * grad
     new_two = 0.999 * moment_two + 0.001 * grad * grad

time: 146 us -> 146 us (level)
  Pallas kernels: 17.2 us -> 11.5 us
  blocking collectives: 112 us -> 117 us
    all_to_all x2, blocking collectives: 29.4 us -> 36.8 us  [the longest x1 27.4 us: per_device(): lax.all_to_all(part, axes, 0, 0, axis_index_groups=over_x[0] + over_z[1],...]
    pallas_call x1, Pallas kernels: 17.2 us -> 11.5 us  [per_device(): pl.pallas_call(grad_kernel, out_shape=jax.ShapeDtypeStruct((x_n, zs, own_...]
    all_to_all x4, blocking collectives: 82.8 us -> 80.7 us  [to_all(): lax.all_to_all(jnp.broadcast_to(array[None], (count, *array.shape)), axes...]
where the time goes in v5:
time: 146 us; the launch traced here: 145 us
  blocking collectives  117 us (80%)
  Pallas kernels  11.5 us (8%)
  starting transfers between devices  8.98 us (6%)
  other arithmetic  2.58 us (2%)
  waiting for transfers between devices  2.25 us (2%)
  local copies, waits for them, and re-layouts  1.92 us (1%)
    all_to_all x4, blocking collectives, to_all(): lax.all_to_all(jnp.broadcast_to(array[None], (count, *array.shape)), axes...  80.7 us
    all_to_all x1, blocking collectives, per_device(): lax.all_to_all(part, axes, 0, 0, axis_index_groups=over_x[0] + over_z[1],...  27.4 us
    pallas_call x1, Pallas kernels, per_device(): pl.pallas_call(grad_kernel, out_shape=jax.ShapeDtypeStruct((x_n, zs, own_...  11.5 us
    all_to_all x1, blocking collectives, per_device(): lax.all_to_all(terms, axes, 0, 0, axis_index_groups=over_z[0] + over_x[1]...  9.34 us
    ppermute x1, starting transfers between devices, per_device(): other = lax.ppermute(along_y, 'c', SWAP)  8.98 us
  transfers between devices with their start and end apart: 1, of which 1 were waited for; matrix products, arithmetic and copies ran while one was open for 0% of the time, Pallas kernels for 0%

profile of v5, /device:TPU:1, one launch (start us, length us, event | category | flops | bytes accessed | tf_op | source)
XLA Modules:
  0.0 145.5 jit_solution(7134274200860900935)
XLA Ops:
  0.6 0.7 select_convert_fusion
  1.4 0.8 pad_maximum_fusion
  2.2 30.1 %all_to_all.30 = bf16[4,72,512]{2,1,0:T(8,128)(2,1)S(1)} all-to-all(bf16[4,72,512]{2,1,0:T(8,128)(2,1)S(1)} %broadcast_in_dim.13), channel_id=1, replica_groups=mesh['x'=4,'zf'=2,'zm'=2,'zp'=2,'y'=4,'zh'=2,'c'=2] {'zf','zh'}, dimensions={0} | all-to-all | bytes 589824 | tf_op jit(solution)/shard_map/all_to_all | solution.py:78
  32.3 0.0 copy-start
  32.3 0.1 broadcast_in_dim.14
  32.4 13.9 %all_to_all.31.own = bf16[4,2,2,64,512]{4,3,2,1,0:T(8,128)(2,1)S(1)} all-to-all(bf16[4,2,2,64,512]{4,3,2,1,0:T(8,128)(2,1)S(1)} %broadcast_in_dim.14), channel_id=1, replica_groups=mesh['x'=4,'zf'=2,'zm'=2,'zp'=2,'y'=4,'zh'=2,'c'=2] {'y'}, dimensions={0} | all-to-all | bytes 2097152 | tf_op jit(solution)/shard_map/all_to_all | solution.py:78
  46.3 9.0 %collective-permute-start = (bf16[4,2,2,64,512]{4,3,2,1,0:T(8,128)(2,1)S(1)}, bf16[4,2,2,64,512]{4,3,2,1,0:T(8,128)(2,1)S(1)}, u32[]{:S(2)}, u32[]{:S(2)}) collective-permute-start(bf16[4,2,2,64,512]{4,3,2,1,0:T(8,128)(2,1)S(1)} %all_to_all.31.own), channel_id=1, source_target_pairs={{0,1},{1,0},{2,3},{3,2},{4,5},{5,4},{6,7},{7,6},{8,9},{9,8},{10,11... | collective-permute-start | bytes 3145736 | tf_op jit(solution)/shard_map/ppermute | solution.py:99
  55.3 2.3 %collective-permute-done.other = bf16[4,2,2,64,512]{4,3,2,1,0:T(8,128)(2,1)S(1)} collective-permute-done((bf16[4,2,2,64,512]{4,3,2,1,0:T(8,128)(2,1)S(1)}, bf16[4,2,2,64,512]{4,3,2,1,0:T(8,128)(2,1)S(1)}, u32[]{:S(2)}, u32[]{:S(2)}) %collective-permute-start) | collective-permute-done | bytes 1048608 | tf_op jit(solution)/shard_map/ppermute | solution.py:99
  57.6 0.0 copy-done
  57.6 11.5 %shard_map.102 = bf16[4,4,32,1024]{3,2,1,0:T(8,128)(2,1)S(1)} custom-call(bf16[4,2,2,64,512]{4,3,2,1,0:T(8,128)(2,1)S(1)} %all_to_all.31.own, bf16[4,2,2,64,512]{4,3,2,1,0:T(8,128)(2,1)S(1)} %collective-permute-done.other, bf16[2,2,8,512]{3,2,1,0:T(8,128)(2,1)S(1)} %slice.41.ids, bf16[4,2,128,1024]{3,2,1,0:T(8,128)(2,1)S(1)} %bitcast.20), custom_call_target="tpu_custom_call" | custom-call | flops 2147483648 | bytes 6291456 | tf_op jit(solution)/shard_map/pallas_call | solution.py:104
  69.1 0.0 copy-start.1
  69.1 0.0 copy-start.2
  69.1 0.0 copy-start.3
  69.1 27.4 %all_to_all.32 = bf16[4,4,32,1024]{3,2,1,0:T(8,128)(2,1)S(1)} all-to-all(bf16[4,4,32,1024]{3,2,1,0:T(8,128)(2,1)S(1)} %shard_map.102), channel_id=1, replica_groups={{0,128,256,384},{16,144,272,400},{32,160,288,416},{48,176,304,432},{1,1..., dimensions={0} | all-to-all | bytes 2097152 | tf_op jit(solution)/shard_map/all_to_all | solution.py:126
  96.6 0.2 fusion
  96.7 9.3 %all_to_all.33 = bf16[4,32,1024]{2,1,0:T(8,128)(2,1)S(1)} all-to-all(bf16[4,32,1024]{2,1,0:T(8,128)(2,1)S(1)} %fusion), channel_id=1, replica_groups={{0,16,32,48},{128,144,160,176},{256,272,288,304},{384,400,416,432},{1,1..., dimensions={0} | all-to-all | bytes 524288 | tf_op jit(solution)/shard_map/all_to_all | solution.py:130
  106.1 0.0 copy-done.1
  106.1 0.0 copy-done.2
  106.1 0.0 copy-done.3
  106.1 0.8 fusion.3
  106.9 14.4 %all_to_all.34 = bf16[4,32,1024]{2,1,0:T(8,128)(2,1)S(1)} all-to-all(bf16[4,32,1024]{2,1,0:T(8,128)(2,1)S(1)} %broadcast_in_dim.15), channel_id=1, replica_groups=mesh['x'=4,'zf'=2,'zm'=2,'zp'=2,'y'=4,'zh'=2,'c'=2] {'zf','zm'}, dimensions={0} | all-to-all | bytes 524288 | tf_op jit(solution)/shard_map/all_to_all | solution.py:78
  121.4 0.3 broadcast_in_dim.16
  121.6 22.4 %all_to_all.35 = bf16[8,4,32,1024]{3,2,1,0:T(8,128)(2,1)S(1)} all-to-all(bf16[8,4,32,1024]{3,2,1,0:T(8,128)(2,1)S(1)} %broadcast_in_dim.16), channel_id=1, replica_groups=mesh['x'=4,'zf'=2,'zm'=2,'zp'=2,'y'=4,'zh'=2,'c'=2] {'x','zp'}, dimensions={0} | all-to-all | bytes 4194304 | tf_op jit(solution)/shard_map/all_to_all | solution.py:78
  144.0 1.5 %copy.11 = bf16[4,4,2,32,1024]{4,3,2,1,0:T(8,128)(2,1)} copy(bf16[4,4,2,32,1024]{4,3,1,2,0:T(8,128)(2,1)S(1)} %bitcast.21) | data formatting | bytes 4194304 | tf_op jit(solution)/shard_map/transpose | solution.py:144
  (4 shorter events, 0.1 us)
Async XLA Ops:
  32.3 25.2 %copy-start = (bf16[1024,1024]{1,0:T(8,128)(2,1)S(1)}, bf16[1024,1024]{1,0:T(8,128)(2,1)}, u32[]{:S(2)}) copy-start(bf16[1024,1024]{1,0:T(8,128)(2,1)} %param.10) | copy-start | bytes 6291460
  46.3 11.3 %collective-permute-start = (bf16[4,2,2,64,512]{4,3,2,1,0:T(8,128)(2,1)S(1)}, bf16[4,2,2,64,512]{4,3,2,1,0:T(8,128)(2,1)S(1)}, u32[]{:S(2)}, u32[]{:S(2)}) collective-permute-start(bf16[4,2,2,64,512]{4,3,2,1,0:T(8,128)(2,1)S(1)} %all_to_all.31.own), channel_id=1, source_target_pairs={{0,1},{1,0},{2,3},{3,2},{4,5},{5,4},{6,7},{7,6},{8,9},{9,8},{10,11... | collective-permute-start | bytes 3145736 | tf_op jit(solution)/shard_map/ppermute | solution.py:99
  69.1 37.0 %copy-start.1 = (f32[32,1024]{1,0:T(8,128)S(1)}, f32[32,1024]{1,0:T(8,128)}, u32[]{:S(2)}) copy-start(f32[32,1024]{1,0:T(8,128)} %param.11) | copy-start | bytes 393220
  69.1 37.0 %copy-start.2 = (f32[32,1024]{1,0:T(8,128)S(1)}, f32[32,1024]{1,0:T(8,128)}, u32[]{:S(2)}) copy-start(f32[32,1024]{1,0:T(8,128)} %param.12) | copy-start | bytes 393220
  69.1 37.0 %copy-start.3 = (f32[32,1024]{1,0:T(8,128)S(1)}, f32[32,1024]{1,0:T(8,128)}, u32[]{:S(2)}) copy-start(f32[32,1024]{1,0:T(8,128)} %param.13) | copy-start | bytes 393220

commit v6 on v4

v6 whole, which is shorter than its diff:
```python
import jax
import jax.numpy as jnp
from jax import lax
from jax.experimental import pallas as pl
from jax.experimental.pallas import tpu as pltpu
from jax.sharding import Mesh
from jax.sharding import PartitionSpec as P

ADAM_STEP = 10
AXES = ("x", "zf", "zm", "zp", "y", "zh", "c")
DP = ("x", "zf", "zm", "zp")
LABEL = ("y", "zh", "c")
SWAP = [(0, 1), (1, 0)]
STAGGER_NS = 10000


def grad_kernel(own, other, weight, out, whole, rows_w, w_sems):
    core, near, zh = lax.axis_index("c"), lax.axis_index("zp"), lax.axis_index("zh")
    label_block = lax.axis_index("y") * 4 + zh * 2 + core
    blocks, ys = own.shape[:2]
    slot_count = 8
    feats = (own.shape[2] - slot_count) // 2
    runs, _, run_rows, width = weight.shape
    rows = runs * run_rows
    fetched = []
    for run in range(runs):
        fetched.append(pltpu.make_async_copy(
            weight.at[run, near], rows_w.at[pl.ds(run * run_rows, run_rows)], w_sems.at[run]))
        fetched[-1].start()
    for y in range(ys):
        for block in range(blocks):
            for swap in range(2):
                half = zh if swap == 0 else 1 - zh
                at = y * 4 * feats + half * 2 * feats
                mine = pl.ds(pl.multiple_of(at + core * feats, feats), feats)
                theirs = pl.ds(pl.multiple_of(at + (1 - core) * feats, feats), feats)
                here = slice(swap * feats, (swap + 1) * feats)
                whole[block, mine, :] = own[block, y, here]
                whole[block, theirs, :] = other[block, y, here]
    row = lax.broadcasted_iota(jnp.int32, (rows, 1), 0)
    first_label = label_block * (2 * rows) + near * run_rows
    label = first_label + (row // run_rows) * (2 * run_rows) + row % run_rows
    for copy in fetched:
        copy.wait()
    total = None
    for block in range(blocks):
        high = own[block, 0, 2 * feats :].astype(jnp.float32)
        low = own[block, 1, 2 * feats :].astype(jnp.float32)
        slots = (high * 128.0 + low).astype(jnp.int32)
        block_q = whole[block]
        logits = jnp.dot(rows_w[...], block_q, preferred_element_type=jnp.float32)
        hit = label == slots[0:1, :]
        for slot in range(1, slot_count):
            hit = hit | (label == slots[slot : slot + 1, :])
        diff = jax.nn.sigmoid(logits) - hit.astype(jnp.float32)
        grad_logit = (diff * (1.0 / 16384)).astype(jnp.bfloat16)
        part = lax.dot_general(
            grad_logit, block_q, (((1,), (1,)), ((), ())), preferred_element_type=jnp.float32
        )
        total = part if total is None else total + part
    out[...] = total.astype(jnp.bfloat16)
    if STAGGER_NS:
        @pl.when(core == 1)
        def _():
            pl.delay(STAGGER_NS)


def summed(terms):
    total = terms[0].astype(jnp.float32)
    for term in range(1, terms.shape[0]):
        total = total + terms[term].astype(jnp.float32)
    return total


def to_all(array, axes):
    count = lax.axis_size(axes)
    return lax.all_to_all(
        jnp.broadcast_to(array[None], (count, *array.shape)), axes, 0, 0, tiled=True
    )


def per_device(queries, positives, counts, weight, master, moment_one, moment_two):
    local_q, feats = queries.shape
    labels, width = weight.shape
    own_rows = master.shape[0]
    x_n, zf_n, zm_n, zp_n = (lax.axis_size(a) for a in DP)
    y_n, zh_n, c_n = (lax.axis_size(a) for a in LABEL)
    zq_n = zf_n * zm_n
    rows = x_n * zq_n * own_rows

    mine = queries.T
    far = lax.ppermute(mine, "zh", SWAP)
    slots = lax.broadcasted_iota(jnp.int32, (positives.shape[1], local_q), 0)
    ids = jnp.where(slots < counts[None, :], positives.T, -1)
    ids = jnp.where(lax.axis_index("y") % 2 == 0, ids >> 7, ids & 127).astype(jnp.bfloat16)
    along_y = to_all(jnp.concatenate([mine, far, ids]), ("zp", "y"))
    along_y = along_y.reshape(zp_n, y_n, 2 * feats + ids.shape[0], local_q)
    other = lax.ppermute(along_y, "c", SWAP)

    vmem = pl.BlockSpec(memory_space=pltpu.VMEM)
    anywhere = pl.BlockSpec(memory_space=pl.ANY)
    part = pl.pallas_call(
        grad_kernel,
        out_shape=jax.ShapeDtypeStruct((rows, width), jnp.bfloat16),
        in_specs=[vmem, vmem, anywhere],
        out_specs=vmem,
        scratch_shapes=[
            pltpu.VMEM((zp_n, width, local_q), jnp.bfloat16),
            pltpu.VMEM((rows, width), jnp.bfloat16),
            pltpu.SemaphoreType.DMA((x_n * zq_n,)),
        ],
        compiler_params=pltpu.CompilerParams(vmem_limit_bytes=32 << 20),
        cost_estimate=pl.CostEstimate(
            flops=4 * rows * width * zp_n * local_q, bytes_accessed=6 << 20, transcendentals=0
        ),
    )(along_y, other, weight.reshape(x_n * zq_n, zp_n, own_rows, width))

    by_x = lax.all_to_all(part.reshape(x_n, zq_n * own_rows, width), "x", 0, 0, tiled=True)
    by_x = summed(by_x).astype(jnp.bfloat16)
    by_z = lax.all_to_all(
        by_x.reshape(zq_n, own_rows, width), ("zf", "zm"), 0, 0, tiled=True
    )
    grad = summed(by_z)

    new_one = 0.9 * moment_one + 0.1 * grad
    new_two = 0.999 * moment_two + 0.001 * grad * grad
    first = new_one / (1.0 - 0.9**ADAM_STEP)
    second = new_two / (1.0 - 0.999**ADAM_STEP)
    new_master = master - 0.02 * (first / (jnp.sqrt(second) + 1e-08) + 0.01 * master)
    low = new_master.astype(jnp.bfloat16)

    every = to_all(to_all(low, ("zf", "zm")), ("x", "zp"))
    every = every.reshape(x_n, zp_n, zf_n * zm_n, own_rows, width)
    new_weight = every.transpose(0, 2, 1, 3, 4).reshape(labels, width)
    return (new_weight, new_master, new_one, new_two)


def solution(mesh):
    torus = Mesh(mesh.devices.reshape(4, 2, 2, 2, 4, 2, 2), AXES)
    in_specs = (
        P(DP, LABEL),
        P(DP, None),
        P(DP),
        P(LABEL, None),
        P(LABEL + DP, None),
        P(LABEL + DP, None),
        P(LABEL + DP, None),
    )
    out_specs = (P(LABEL, None),) + (P(LABEL + DP, None),) * 3
    return jax.shard_map(
        per_device, mesh=torus, in_specs=in_specs, out_specs=out_specs, check_vma=False
    )
```

time: 146 us -> 140 us (0.959)
  blocking collectives: 112 us -> 92.8 us
  starting transfers between devices: 8.98 us -> 22.8 us
  Pallas kernels: 17.2 us -> 14.9 us
    all_to_all x4 -> x3, blocking collectives: 82.8 us -> 56.1 us  [to_all(): lax.all_to_all(jnp.broadcast_to(array[None], (count, *array.shape)), axes...]
    ppermute x0 -> x1, starting transfers between devices: none -> 16.4 us  [per_device(): far = lax.ppermute(mine, 'zh', SWAP)]
    all_to_all x2, blocking collectives: 29.4 us -> 36.7 us  [the longest x1 23 us: per_device(): lax.all_to_all(by_x.reshape(zq_n, own_rows, width), ('zf', 'zm'), 0, 0, t...]
    ppermute x1, starting transfers between devices: 8.98 us -> 6.38 us  [per_device(): other = lax.ppermute(along_y, 'c', SWAP)]
    pallas_call x1, Pallas kernels: 17.2 us -> 14.9 us  [per_device(): pl.pallas_call(grad_kernel, out_shape=jax.ShapeDtypeStruct((rows, width),...]
  transfers between devices with their start and end apart: 1 -> 2, of which waited for: 1 -> 2; matrix products, arithmetic and copies ran while one was open for 0% -> 1% of each run, Pallas kernels for 0% -> 0%
where the time goes in v6:
time: 140 us; the launch traced here: 139 us
  blocking collectives  92.8 us (66%)
  starting transfers between devices  22.8 us (16%)
  Pallas kernels  14.9 us (11%)
  waiting for transfers between devices  3.67 us (3%)
  other arithmetic  2.58 us (2%)
  local copies, waits for them, and re-layouts  1.86 us (1%)
    all_to_all x3, blocking collectives, to_all(): lax.all_to_all(jnp.broadcast_to(array[None], (count, *array.shape)), axes...  56.1 us
    all_to_all x1, blocking collectives, per_device(): lax.all_to_all(by_x.reshape(zq_n, own_rows, width), ('zf', 'zm'), 0, 0, t...  23 us
    ppermute x1, starting transfers between devices, per_device(): far = lax.ppermute(mine, 'zh', SWAP)  16.4 us
    pallas_call x1, Pallas kernels, per_device(): pl.pallas_call(grad_kernel, out_shape=jax.ShapeDtypeStruct((rows, width),...  14.9 us
    all_to_all x1, blocking collectives, per_device(): lax.all_to_all(part.reshape(x_n, zq_n * own_rows, width), 'x', 0, 0, tile...  13.7 us
    ppermute x1, starting transfers between devices, per_device(): other = lax.ppermute(along_y, 'c', SWAP)  6.38 us
  transfers between devices with their start and end apart: 2, of which 2 were waited for; matrix products, arithmetic and copies ran while one was open for 1% of the time, Pallas kernels for 0%

profile of v6, /device:TPU:1, one launch (start us, length us, event | category | flops | bytes accessed | tf_op | source)
XLA Modules:
  0.0 139.4 jit_solution(12360860334298524230)
XLA Ops:
  0.6 0.0 copy-start
  0.6 16.4 %collective-permute-start = (bf16[64,512]{1,0:T(8,128)(2,1)}, bf16[64,512]{1,0:T(8,128)(2,1)S(1)}, u32[]{:S(2)}, u32[]{:S(2)}) collective-permute-start(bf16[64,512]{1,0:T(8,128)(2,1)} %bitcast.27), channel_id=1, source_target_pairs={{0,2},{2,0},{1,3},{3,1},{4,6},{6,4},{5,7},{7,5},{8,10},{10,8},{9,1... | collective-permute-start | bytes 196616 | tf_op jit(solution)/shard_map/ppermute | solution.py:92
  17.1 0.7 select_convert_fusion
  17.8 1.3 collective-permute-done
  19.1 0.8 pad_maximum_fusion
  20.0 0.1 broadcast_in_dim.11
  20.0 17.2 %all_to_all.25 = bf16[8,136,512]{2,1,0:T(8,128)(2,1)S(1)} all-to-all(bf16[8,136,512]{2,1,0:T(8,128)(2,1)S(1)} %broadcast_in_dim.11), channel_id=1, replica_groups=mesh['x'=4,'zf'=2,'zm'=2,'zp'=2,'y'=4,'zh'=2,'c'=2] {'zp','y'}, dimensions={0} | all-to-all | bytes 2228224 | tf_op jit(solution)/shard_map/all_to_all | solution.py:77
  37.3 6.4 %collective-permute-start.1 = (bf16[2,4,136,512]{3,2,1,0:T(8,128)(2,1)S(1)}, bf16[2,4,136,512]{3,2,1,0:T(8,128)(2,1)S(1)}, u32[]{:S(2)}, u32[]{:S(2)}) collective-permute-start(bf16[2,4,136,512]{3,2,1,0:T(8,128)(2,1)S(1)} %bitcast.20), channel_id=1, source_target_pairs={{0,1},{1,0},{2,3},{3,2},{4,5},{5,4},{6,7},{7,6},{8,9},{9,8},{10,11... | collective-permute-start | bytes 3342344 | tf_op jit(solution)/shard_map/ppermute | solution.py:98
  43.6 2.4 %collective-permute-done.1.other = bf16[2,4,136,512]{3,2,1,0:T(8,128)(2,1)S(1)} collective-permute-done((bf16[2,4,136,512]{3,2,1,0:T(8,128)(2,1)S(1)}, bf16[2,4,136,512]{3,2,1,0:T(8,128)(2,1)S(1)}, u32[]{:S(2)}, u32[]{:S(2)}) %collective-permute-start.1) | collective-permute-done | bytes 1114144 | tf_op jit(solution)/shard_map/ppermute | solution.py:98
  46.0 0.0 copy-done
  46.0 14.9 %shard_map.102 = bf16[512,1024]{1,0:T(8,128)(2,1)S(1)} custom-call(bf16[2,4,136,512]{3,2,1,0:T(8,128)(2,1)S(1)} %bitcast.21, bf16[2,4,136,512]{3,2,1,0:T(8,128)(2,1)S(1)} %collective-permute-done.1.other, bf16[16,2,32,1024]{3,2,1,0:T(8,128)(2,1)S(1)} %bitcast.23), custom_call_target="tpu_custom_call" | custom-call | flops 2147483648 | bytes 6291456 | tf_op jit(solution)/shard_map/pallas_call | solution.py:102
  60.9 0.0 copy-start.1
  61.0 0.0 copy-start.2
  61.0 0.0 copy-start.3
  61.0 13.7 %all_to_all.26 = bf16[4,128,1024]{2,1,0:T(8,128)(2,1)S(1)} all-to-all(bf16[4,128,1024]{2,1,0:T(8,128)(2,1)S(1)} %bitcast.22), channel_id=1, replica_groups=mesh['x'=4,'zf'=2,'zm'=2,'zp'=2,'y'=4,'zh'=2,'c'=2] {'x'}, dimensions={0} | all-to-all | bytes 2097152 | tf_op jit(solution)/shard_map/all_to_all | solution.py:118
  74.7 0.2 add_convert_fusion
  74.9 23.0 %all_to_all.27 = bf16[4,32,1024]{2,1,0:T(8,128)(2,1)S(1)} all-to-all(bf16[4,32,1024]{2,1,0:T(8,128)(2,1)S(1)} %bitcast.26), channel_id=1, replica_groups=mesh['x'=4,'zf'=2,'zm'=2,'zp'=2,'y'=4,'zh'=2,'c'=2] {'zf','zm'}, dimensions={0} | all-to-all | bytes 524288 | tf_op jit(solution)/shard_map/all_to_all | solution.py:120
  97.9 0.0 copy-done.1
  97.9 0.0 copy-done.2
  97.9 0.0 copy-done.3
  97.9 0.8 fusion.2
  98.7 14.3 %all_to_all.28 = bf16[4,32,1024]{2,1,0:T(8,128)(2,1)S(1)} all-to-all(bf16[4,32,1024]{2,1,0:T(8,128)(2,1)S(1)} %broadcast_in_dim.12), channel_id=1, replica_groups=mesh['x'=4,'zf'=2,'zm'=2,'zp'=2,'y'=4,'zh'=2,'c'=2] {'zf','zm'}, dimensions={0} | all-to-all | bytes 524288 | tf_op jit(solution)/shard_map/all_to_all | solution.py:77
  113.1 0.3 broadcast_in_dim.13
  113.3 24.5 %all_to_all.29 = bf16[8,4,32,1024]{3,2,1,0:T(8,128)(2,1)S(1)} all-to-all(bf16[8,4,32,1024]{3,2,1,0:T(8,128)(2,1)S(1)} %broadcast_in_dim.13), channel_id=1, replica_groups=mesh['x'=4,'zf'=2,'zm'=2,'zp'=2,'y'=4,'zh'=2,'c'=2] {'x','zp'}, dimensions={0} | all-to-all | bytes 4194304 | tf_op jit(solution)/shard_map/all_to_all | solution.py:77
  137.9 1.5 %copy.11 = bf16[4,4,2,32,1024]{4,3,2,1,0:T(8,128)(2,1)} copy(bf16[4,4,2,32,1024]{4,3,1,2,0:T(8,128)(2,1)S(1)} %bitcast.24) | data formatting | bytes 4194304 | tf_op jit(solution)/shard_map/transpose | solution.py:134
  (1 shorter events, 0.0 us)
Async XLA Ops:
  0.6 45.4 %copy-start = (bf16[1024,1024]{1,0:T(8,128)(2,1)S(1)}, bf16[1024,1024]{1,0:T(8,128)(2,1)}, u32[]{:S(2)}) copy-start(bf16[1024,1024]{1,0:T(8,128)(2,1)} %param.10) | copy-start | bytes 6291460
  0.6 18.5 %collective-permute-start = (bf16[64,512]{1,0:T(8,128)(2,1)}, bf16[64,512]{1,0:T(8,128)(2,1)S(1)}, u32[]{:S(2)}, u32[]{:S(2)}) collective-permute-start(bf16[64,512]{1,0:T(8,128)(2,1)} %bitcast.27), channel_id=1, source_target_pairs={{0,2},{2,0},{1,3},{3,1},{4,6},{6,4},{5,7},{7,5},{8,10},{10,8},{9,1... | collective-permute-start | bytes 196616 | tf_op jit(solution)/shard_map/ppermute | solution.py:92
  37.3 8.7 %collective-permute-start.1 = (bf16[2,4,136,512]{3,2,1,0:T(8,128)(2,1)S(1)}, bf16[2,4,136,512]{3,2,1,0:T(8,128)(2,1)S(1)}, u32[]{:S(2)}, u32[]{:S(2)}) collective-permute-start(bf16[2,4,136,512]{3,2,1,0:T(8,128)(2,1)S(1)} %bitcast.20), channel_id=1, source_target_pairs={{0,1},{1,0},{2,3},{3,2},{4,5},{5,4},{6,7},{7,6},{8,9},{9,8},{10,11... | collective-permute-start | bytes 3342344 | tf_op jit(solution)/shard_map/ppermute | solution.py:98
  60.9 36.9 %copy-start.1 = (f32[32,1024]{1,0:T(8,128)S(1)}, f32[32,1024]{1,0:T(8,128)}, u32[]{:S(2)}) copy-start(f32[32,1024]{1,0:T(8,128)} %param.11) | copy-start | bytes 393220
  61.0 36.9 %copy-start.2 = (f32[32,1024]{1,0:T(8,128)S(1)}, f32[32,1024]{1,0:T(8,128)}, u32[]{:S(2)}) copy-start(f32[32,1024]{1,0:T(8,128)} %param.12) | copy-start | bytes 393220
  61.0 36.9 %copy-start.3 = (f32[32,1024]{1,0:T(8,128)S(1)}, f32[32,1024]{1,0:T(8,128)}, u32[]{:S(2)}) copy-start(f32[32,1024]{1,0:T(8,128)} %param.13) | copy-start | bytes 393220

commit v7 on v6

--- a/solution.py
+++ b/solution.py
@@ -14,7 +14,7 @@
 STAGGER_NS = 10000
 
 
-def grad_kernel(own, other, weight, out, whole, rows_w, w_sems):
+def grad_kernel(own, other, weight, out, whole, rows_w):
     core, near, zh = lax.axis_index("c"), lax.axis_index("zp"), lax.axis_index("zh")
     label_block = lax.axis_index("y") * 4 + zh * 2 + core
     blocks, ys = own.shape[:2]
@@ -22,11 +22,8 @@
     feats = (own.shape[2] - slot_count) // 2
     runs, _, run_rows, width = weight.shape
     rows = runs * run_rows
-    fetched = []
     for run in range(runs):
-        fetched.append(pltpu.make_async_copy(
-            weight.at[run, near], rows_w.at[pl.ds(run * run_rows, run_rows)], w_sems.at[run]))
-        fetched[-1].start()
+        rows_w[pl.ds(run * run_rows, run_rows), :] = weight[run, near]
     for y in range(ys):
         for block in range(blocks):
             for swap in range(2):
@@ -40,8 +37,6 @@
     row = lax.broadcasted_iota(jnp.int32, (rows, 1), 0)
     first_label = label_block * (2 * rows) + near * run_rows
     label = first_label + (row // run_rows) * (2 * run_rows) + row % run_rows
-    for copy in fetched:
-        copy.wait()
     total = None
     for block in range(blocks):
         high = own[block, 0, 2 * feats :].astype(jnp.float32)
@@ -63,6 +58,27 @@
         @pl.when(core == 1)
         def _():
             pl.delay(STAGGER_NS)
+
+
+def pack_kernel(mine, far, ids, out):
+    feats = mine.shape[0]
+    for copy in range(out.shape[0]):
+        out[copy, 0:feats] = mine[...]
+        out[copy, feats : 2 * feats] = far[...]
+        out[copy, 2 * feats :] = ids[...]
+
+
+def place_kernel(every, out, sems):
+    xs, zps, zqs = every.shape[:3]
+    copies = []
+    for x in range(xs):
+        for zp in range(zps):
+            for zq in range(zqs):
+                copies.append(pltpu.make_async_copy(
+                    every.at[x, zp, zq], out.at[x, zq, zp], sems.at[x, zp, zq]))
+                copies[-1].start()
+    for copy in copies:
+        copy.wait()
 
 
 def summed(terms):
@@ -93,21 +109,27 @@
     slots = lax.broadcasted_iota(jnp.int32, (positives.shape[1], local_q), 0)
     ids = jnp.where(slots < counts[None, :], positives.T, -1)
     ids = jnp.where(lax.axis_index("y") % 2 == 0, ids >> 7, ids & 127).astype(jnp.bfloat16)
-    along_y = to_all(jnp.concatenate([mine, far, ids]), ("zp", "y"))
-    along_y = along_y.reshape(zp_n, y_n, 2 * feats + ids.shape[0], local_q)
+    vmem = pl.BlockSpec(memory_space=pltpu.VMEM)
+    piece_rows = 2 * feats + ids.shape[0]
+    sent = pl.pallas_call(
+        pack_kernel,
+        out_shape=jax.ShapeDtypeStruct((zp_n * y_n, piece_rows, local_q), jnp.bfloat16),
+        in_specs=[vmem, vmem, vmem],
+        out_specs=vmem,
+        compiler_params=pltpu.CompilerParams(vmem_limit_bytes=16 << 20),
+    )(mine, far, ids)
+    along_y = lax.all_to_all(sent, ("zp", "y"), 0, 0, tiled=True)
+    along_y = along_y.reshape(zp_n, y_n, piece_rows, local_q)
     other = lax.ppermute(along_y, "c", SWAP)
 
-    vmem = pl.BlockSpec(memory_space=pltpu.VMEM)
-    anywhere = pl.BlockSpec(memory_space=pl.ANY)
     part = pl.pallas_call(
         grad_kernel,
         out_shape=jax.ShapeDtypeStruct((rows, width), jnp.bfloat16),
-        in_specs=[vmem, vmem, anywhere],
+        in_specs=[vmem, vmem, vmem],
         out_specs=vmem,
         scratch_shapes=[
             pltpu.VMEM((zp_n, width, local_q), jnp.bfloat16),
             pltpu.VMEM((rows, width), jnp.bfloat16),
-            pltpu.SemaphoreType.DMA((x_n * zq_n,)),
         ],
         compiler_params=pltpu.CompilerParams(vmem_limit_bytes=32 << 20),
         cost_estimate=pl.CostEstimate(
@@ -130,8 +152,14 @@
     low = new_master.astype(jnp.bfloat16)
 
     every = to_all(to_all(low, ("zf", "zm")), ("x", "zp"))
-    every = every.reshape(x_n, zp_n, zf_n * zm_n, own_rows, width)
-    new_weight = every.transpose(0, 2, 1, 3, 4).reshape(labels, width)
+    new_weight = pl.pallas_call(
+        place_kernel,
+        out_shape=jax.ShapeDtypeStruct((x_n, zq_n, zp_n, own_rows, width), jnp.bfloat16),
+        in_specs=[vmem],
+        out_specs=pl.BlockSpec(memory_space=pl.ANY),
+        scratch_shapes=[pltpu.SemaphoreType.DMA((x_n, zp_n, zq_n))],
+        compiler_params=pltpu.CompilerParams(vmem_limit_bytes=16 << 20),
+    )(every.reshape(x_n, zp_n, zq_n, own_rows, width)).reshape(labels, width)
     return (new_weight, new_master, new_one, new_two)
 
 

time: 140 us -> 138 us (0.986)
  blocking collectives: 92.8 us -> 103 us
  Pallas kernels: 14.9 us -> 4.93 us
    all_to_all x0 -> x1, blocking collectives: none -> 17.4 us  [per_device(): along_y = lax.all_to_all(sent, ('zp', 'y'), 0, 0, tiled=True)]
    all_to_all x3 -> x2, blocking collectives: 56.1 us -> 38.9 us  [to_all(): lax.all_to_all(jnp.broadcast_to(array[None], (count, *array.shape)), axes...]
    pallas_call x1, Pallas kernels: 14.9 us -> 3.29 us  [per_device(): pl.pallas_call(grad_kernel, out_shape=jax.ShapeDtypeStruct((rows, width),...]
    all_to_all x1, blocking collectives: 13.7 us -> 23.7 us  [per_device(): lax.all_to_all(part.reshape(x_n, zq_n * own_rows, width), 'x', 0, 0, tile...]
    pallas_call x0 -> x2, Pallas kernels: none -> 1.64 us  [the longest x1 1.57 us: per_device(): pl.pallas_call(place_kernel, out_shape=jax.ShapeDtypeStruct((x_n, zq_n, z...]
    transpose x1 -> x0, local copies, waits for them, and re-layouts: 1.49 us -> none  [per_device(): new_weight = every.transpose(0, 2, 1, 3, 4).reshape(labels, width)]
where the time goes in v7:
time: 138 us
  blocking collectives  103 us (75%)
  starting transfers between devices  22.6 us (16%)
  Pallas kernels  4.93 us (4%)
  waiting for transfers between devices  3.67 us (3%)
  other arithmetic  1.73 us (1%)
    all_to_all x2, blocking collectives, to_all(): lax.all_to_all(jnp.broadcast_to(array[None], (count, *array.shape)), axes...  38.9 us
    all_to_all x1, blocking collectives, per_device(): lax.all_to_all(part.reshape(x_n, zq_n * own_rows, width), 'x', 0, 0, tile...  23.7 us
    all_to_all x1, blocking collectives, per_device(): lax.all_to_all(by_x.reshape(zq_n, own_rows, width), ('zf', 'zm'), 0, 0, t...  23 us
    all_to_all x1, blocking collectives, per_device(): along_y = lax.all_to_all(sent, ('zp', 'y'), 0, 0, tiled=True)  17.4 us
    ppermute x1, starting transfers between devices, per_device(): far = lax.ppermute(mine, 'zh', SWAP)  16.3 us
    ppermute x1, starting transfers between devices, per_device(): other = lax.ppermute(along_y, 'c', SWAP)  6.38 us
    pallas_call x1, Pallas kernels, per_device(): pl.pallas_call(grad_kernel, out_shape=jax.ShapeDtypeStruct((rows, width),...  3.29 us
  transfers between devices with their start and end apart: 2, of which 2 were waited for; matrix products, arithmetic and copies ran while one was open for 1% of the time, Pallas kernels for 0%

profile of v7, /device:TPU:1, one launch (start us, length us, event | category | flops | bytes accessed | tf_op | source)
XLA Modules:
  0.0 137.8 jit_solution(5502092484755448764)
XLA Ops:
  0.6 16.3 %collective-permute-start = (bf16[64,512]{1,0:T(8,128)(2,1)}, bf16[64,512]{1,0:T(8,128)(2,1)S(1)}, u32[]{:S(2)}, u32[]{:S(2)}) collective-permute-start(bf16[64,512]{1,0:T(8,128)(2,1)} %bitcast.22), channel_id=1, source_target_pairs={{0,2},{2,0},{1,3},{3,1},{4,6},{6,4},{5,7},{7,5},{8,10},{10,8},{9,1... | collective-permute-start | bytes 196616 | tf_op jit(solution)/shard_map/ppermute | solution.py:108
  16.9 0.7 select_convert_fusion.ids
  17.6 1.3 collective-permute-done.far
  19.0 0.0 copy-start
  19.0 0.8 copy-done
  19.8 0.0 copy-start.1
  19.8 0.1 shard_map.102
  19.9 17.4 %all_to_all.25 = bf16[8,136,512]{2,1,0:T(8,128)(2,1)S(1)} all-to-all(bf16[8,136,512]{2,1,0:T(8,128)(2,1)S(1)} %shard_map.102), channel_id=1, replica_groups=mesh['x'=4,'zf'=2,'zm'=2,'zp'=2,'y'=4,'zh'=2,'c'=2] {'zp','y'}, dimensions={0} | all-to-all | bytes 2228224 | tf_op jit(solution)/shard_map/all_to_all | solution.py:121
  37.2 6.4 %collective-permute-start.1 = (bf16[2,4,136,512]{3,2,1,0:T(8,128)(2,1)S(1)}, bf16[2,4,136,512]{3,2,1,0:T(8,128)(2,1)S(1)}, u32[]{:S(2)}, u32[]{:S(2)}) collective-permute-start(bf16[2,4,136,512]{3,2,1,0:T(8,128)(2,1)S(1)} %bitcast.19), channel_id=1, source_target_pairs={{0,1},{1,0},{2,3},{3,2},{4,5},{5,4},{6,7},{7,6},{8,9},{9,8},{10,11... | collective-permute-start | bytes 3342344 | tf_op jit(solution)/shard_map/ppermute | solution.py:123
  43.6 2.4 %collective-permute-done.1.other = bf16[2,4,136,512]{3,2,1,0:T(8,128)(2,1)S(1)} collective-permute-done((bf16[2,4,136,512]{3,2,1,0:T(8,128)(2,1)S(1)}, bf16[2,4,136,512]{3,2,1,0:T(8,128)(2,1)S(1)}, u32[]{:S(2)}, u32[]{:S(2)}) %collective-permute-start.1) | collective-permute-done | bytes 1114144 | tf_op jit(solution)/shard_map/ppermute | solution.py:123
  46.0 0.0 copy-done.1
  46.0 3.3 %shard_map.103 = bf16[512,1024]{1,0:T(8,128)(2,1)S(1)} custom-call(bf16[2,4,136,512]{3,2,1,0:T(8,128)(2,1)S(1)} %bitcast.20, bf16[2,4,136,512]{3,2,1,0:T(8,128)(2,1)S(1)} %collective-permute-done.1.other, bf16[16,2,32,1024]{3,2,1,0:T(8,128)(2,1)S(1)} %bitcast.24), custom_call_target="tpu_custom_call" | custom-call | flops 2147483648 | bytes 6291456 | tf_op jit(solution)/shard_map/pallas_call | solution.py:125
  49.3 0.0 copy-start.2
  49.3 0.0 copy-start.3
  49.3 0.0 copy-start.4
  49.3 23.7 %all_to_all.26 = bf16[4,128,1024]{2,1,0:T(8,128)(2,1)S(1)} all-to-all(bf16[4,128,1024]{2,1,0:T(8,128)(2,1)S(1)} %bitcast.21), channel_id=1, replica_groups=mesh['x'=4,'zf'=2,'zm'=2,'zp'=2,'y'=4,'zh'=2,'c'=2] {'x'}, dimensions={0} | all-to-all | bytes 2097152 | tf_op jit(solution)/shard_map/all_to_all | solution.py:140
  73.0 0.2 add_convert_fusion
  73.2 23.0 %all_to_all.27 = bf16[4,32,1024]{2,1,0:T(8,128)(2,1)S(1)} all-to-all(bf16[4,32,1024]{2,1,0:T(8,128)(2,1)S(1)} %bitcast.26), channel_id=1, replica_groups=mesh['x'=4,'zf'=2,'zm'=2,'zp'=2,'y'=4,'zh'=2,'c'=2] {'zf','zm'}, dimensions={0} | all-to-all | bytes 524288 | tf_op jit(solution)/shard_map/all_to_all | solution.py:142
  96.2 0.0 copy-done.2
  96.2 0.0 copy-done.3
  96.2 0.0 copy-done.4
  96.2 0.8 fusion.2
  97.0 14.3 %all_to_all.28 = bf16[4,32,1024]{2,1,0:T(8,128)(2,1)S(1)} all-to-all(bf16[4,32,1024]{2,1,0:T(8,128)(2,1)S(1)} %broadcast_in_dim.9), channel_id=1, replica_groups=mesh['x'=4,'zf'=2,'zm'=2,'zp'=2,'y'=4,'zh'=2,'c'=2] {'zf','zm'}, dimensions={0} | all-to-all | bytes 524288 | tf_op jit(solution)/shard_map/all_to_all | solution.py:93
  111.4 0.3 broadcast_in_dim.10
  111.6 24.6 %all_to_all.29 = bf16[8,4,32,1024]{3,2,1,0:T(8,128)(2,1)S(1)} all-to-all(bf16[8,4,32,1024]{3,2,1,0:T(8,128)(2,1)S(1)} %broadcast_in_dim.10), channel_id=1, replica_groups=mesh['x'=4,'zf'=2,'zm'=2,'zp'=2,'y'=4,'zh'=2,'c'=2] {'x','zp'}, dimensions={0} | all-to-all | bytes 4194304 | tf_op jit(solution)/shard_map/all_to_all | solution.py:93
  136.2 1.6 %shard_map.104 = bf16[4,4,2,32,1024]{4,3,2,1,0:T(8,128)(2,1)} custom-call(bf16[4,2,4,32,1024]{4,3,2,1,0:T(8,128)(2,1)S(1)} %bitcast.18), custom_call_target="tpu_custom_call" | custom-call | tf_op jit(solution)/shard_map/pallas_call | solution.py:155
  (1 shorter events, 0.0 us)
Async XLA Ops:
  0.6 18.3 %collective-permute-start = (bf16[64,512]{1,0:T(8,128)(2,1)}, bf16[64,512]{1,0:T(8,128)(2,1)S(1)}, u32[]{:S(2)}, u32[]{:S(2)}) collective-permute-start(bf16[64,512]{1,0:T(8,128)(2,1)} %bitcast.22), channel_id=1, source_target_pairs={{0,2},{2,0},{1,3},{3,1},{4,6},{6,4},{5,7},{7,5},{8,10},{10,8},{9,1... | collective-permute-start | bytes 196616 | tf_op jit(solution)/shard_map/ppermute | solution.py:108
  19.0 0.8 copy-start
  19.8 26.2 %copy-start.1 = (bf16[1024,1024]{1,0:T(8,128)(2,1)S(1)}, bf16[1024,1024]{1,0:T(8,128)(2,1)}, u32[]{:S(2)}) copy-start(bf16[1024,1024]{1,0:T(8,128)(2,1)} %param.10) | copy-start | bytes 6291460
  37.2 8.7 %collective-permute-start.1 = (bf16[2,4,136,512]{3,2,1,0:T(8,128)(2,1)S(1)}, bf16[2,4,136,512]{3,2,1,0:T(8,128)(2,1)S(1)}, u32[]{:S(2)}, u32[]{:S(2)}) collective-permute-start(bf16[2,4,136,512]{3,2,1,0:T(8,128)(2,1)S(1)} %bitcast.19), channel_id=1, source_target_pairs={{0,1},{1,0},{2,3},{3,2},{4,5},{5,4},{6,7},{7,6},{8,9},{9,8},{10,11... | collective-permute-start | bytes 3342344 | tf_op jit(solution)/shard_map/ppermute | solution.py:123
  49.3 46.9 %copy-start.2 = (f32[32,1024]{1,0:T(8,128)S(1)}, f32[32,1024]{1,0:T(8,128)}, u32[]{:S(2)}) copy-start(f32[32,1024]{1,0:T(8,128)} %param.11) | copy-start | bytes 393220
  49.3 46.9 %copy-start.3 = (f32[32,1024]{1,0:T(8,128)S(1)}, f32[32,1024]{1,0:T(8,128)}, u32[]{:S(2)}) copy-start(f32[32,1024]{1,0:T(8,128)} %param.12) | copy-start | bytes 393220
  49.3 46.9 %copy-start.4 = (f32[32,1024]{1,0:T(8,128)S(1)}, f32[32,1024]{1,0:T(8,128)}, u32[]{:S(2)}) copy-start(f32[32,1024]{1,0:T(8,128)} %param.13) | copy-start | bytes 393220

commit v8 on v7

--- a/solution.py
+++ b/solution.py
@@ -60,12 +60,21 @@
             pl.delay(STAGGER_NS)
 
 
-def pack_kernel(mine, far, ids, out):
-    feats = mine.shape[0]
+def base_kernel(mine, positives, counts, out):
+    feats, slot_count = mine.shape[0], positives.shape[0]
+    out[0:feats] = mine[...]
+    slot = lax.broadcasted_iota(jnp.int32, positives.shape, 0)
+    ids = jnp.where(slot < counts[...], positives[...], -1)
+    digit = jnp.where(lax.axis_index("y") % 2 == 0, ids >> 7, ids & 127)
+    out[feats : feats + slot_count] = digit.astype(jnp.float32).astype(jnp.bfloat16)
+
+
+def pack_kernel(base, far, out):
+    feats = far.shape[0]
     for copy in range(out.shape[0]):
-        out[copy, 0:feats] = mine[...]
+        out[copy, 0:feats] = base[0:feats]
         out[copy, feats : 2 * feats] = far[...]
-        out[copy, 2 * feats :] = ids[...]
+        out[copy, 2 * feats :] = base[feats:]
 
 
 def place_kernel(every, out, sems):
@@ -106,18 +115,23 @@
 
     mine = queries.T
     far = lax.ppermute(mine, "zh", SWAP)
-    slots = lax.broadcasted_iota(jnp.int32, (positives.shape[1], local_q), 0)
-    ids = jnp.where(slots < counts[None, :], positives.T, -1)
-    ids = jnp.where(lax.axis_index("y") % 2 == 0, ids >> 7, ids & 127).astype(jnp.bfloat16)
     vmem = pl.BlockSpec(memory_space=pltpu.VMEM)
-    piece_rows = 2 * feats + ids.shape[0]
+    slot_count = positives.shape[1]
+    piece_rows = 2 * feats + slot_count
+    base = pl.pallas_call(
+        base_kernel,
+        out_shape=jax.ShapeDtypeStruct((feats + slot_count, local_q), jnp.bfloat16),
+        in_specs=[vmem, vmem, vmem],
+        out_specs=vmem,
+        compiler_params=pltpu.CompilerParams(vmem_limit_bytes=16 << 20),
+    )(mine, positives.T, counts[None, :])
     sent = pl.pallas_call(
         pack_kernel,
         out_shape=jax.ShapeDtypeStruct((zp_n * y_n, piece_rows, local_q), jnp.bfloat16),
-        in_specs=[vmem, vmem, vmem],
+        in_specs=[vmem, vmem],
         out_specs=vmem,
         compiler_params=pltpu.CompilerParams(vmem_limit_bytes=16 << 20),
-    )(mine, far, ids)
+    )(base, far)
     along_y = lax.all_to_all(sent, ("zp", "y"), 0, 0, tiled=True)
     along_y = along_y.reshape(zp_n, y_n, piece_rows, local_q)
     other = lax.ppermute(along_y, "c", SWAP)

time: 138 us -> 137 us (level)
  local copies, waits for them, and re-layouts: 1.13 us -> 2.53 us
    unnamed x10 -> x14, local copies, waits for them, and re-layouts: 0.86 us -> 2.26 us
  transfers between devices with their start and end apart: 2 -> 2, of which waited for: 2 -> 1; matrix products, arithmetic and copies ran while one was open for 1% -> 0% of each run, Pallas kernels for 0% -> 0%
where the time goes in v8:
time: 137 us
  blocking collectives  103 us (75%)
  starting transfers between devices  22.4 us (16%)
  Pallas kernels  4.97 us (4%)
  local copies, waits for them, and re-layouts  2.53 us (2%)
  waiting for transfers between devices  2.36 us (2%)
    all_to_all x2, blocking collectives, to_all(): lax.all_to_all(jnp.broadcast_to(array[None], (count, *array.shape)), axes...  38.9 us
    all_to_all x1, blocking collectives, per_device(): lax.all_to_all(part.reshape(x_n, zq_n * own_rows, width), 'x', 0, 0, tile...  23.6 us
    all_to_all x1, blocking collectives, per_device(): lax.all_to_all(by_x.reshape(zq_n, own_rows, width), ('zf', 'zm'), 0, 0, t...  22.5 us
    all_to_all x1, blocking collectives, per_device(): along_y = lax.all_to_all(sent, ('zp', 'y'), 0, 0, tiled=True)  17.9 us
    ppermute x1, starting transfers between devices, per_device(): far = lax.ppermute(mine, 'zh', SWAP)  16.3 us
    ppermute x1, starting transfers between devices, per_device(): other = lax.ppermute(along_y, 'c', SWAP)  6.09 us
    pallas_call x1, Pallas kernels, per_device(): pl.pallas_call(grad_kernel, out_shape=jax.ShapeDtypeStruct((rows, width),...  3.31 us
  transfers between devices with their start and end apart: 2, of which 1 were waited for; matrix products, arithmetic and copies ran while one was open for 0% of the time, Pallas kernels for 0%

profile of v8, /device:TPU:1, one launch (start us, length us, event | category | flops | bytes accessed | tf_op | source)
XLA Modules:
  0.0 136.8 jit_solution(12772043824461701263)
XLA Ops:
  0.6 16.3 %collective-permute-start = (bf16[64,512]{1,0:T(8,128)(2,1)}, bf16[64,512]{1,0:T(8,128)(2,1)S(1)}, u32[]{:S(2)}, u32[]{:S(2)}) collective-permute-start(bf16[64,512]{1,0:T(8,128)(2,1)} %bitcast.20), channel_id=1, source_target_pairs={{0,2},{2,0},{1,3},{3,1},{4,6},{6,4},{5,7},{7,5},{8,10},{10,8},{9,1... | collective-permute-start | bytes 196616 | tf_op jit(solution)/shard_map/ppermute | solution.py:117
  16.9 0.0 copy-start
  16.9 0.8 copy-done
  17.8 0.0 copy-start.1
  17.8 0.7 copy-done.1
  18.5 0.0 copy-start.2
  18.5 0.7 copy-done.2
  19.2 0.0 copy-start.3
  19.2 0.0 collective-permute-done.far
  19.2 0.1 shard_map.103
  19.3 17.9 %all_to_all.25 = bf16[8,136,512]{2,1,0:T(8,128)(2,1)S(1)} all-to-all(bf16[8,136,512]{2,1,0:T(8,128)(2,1)S(1)} %shard_map.103), channel_id=1, replica_groups=mesh['x'=4,'zf'=2,'zm'=2,'zp'=2,'y'=4,'zh'=2,'c'=2] {'zp','y'}, dimensions={0} | all-to-all | bytes 2228224 | tf_op jit(solution)/shard_map/all_to_all | solution.py:135
  37.1 6.1 %collective-permute-start.1 = (bf16[2,4,136,512]{3,2,1,0:T(8,128)(2,1)S(1)}, bf16[2,4,136,512]{3,2,1,0:T(8,128)(2,1)S(1)}, u32[]{:S(2)}, u32[]{:S(2)}) collective-permute-start(bf16[2,4,136,512]{3,2,1,0:T(8,128)(2,1)S(1)} %bitcast.17), channel_id=1, source_target_pairs={{0,1},{1,0},{2,3},{3,2},{4,5},{5,4},{6,7},{7,6},{8,9},{9,8},{10,11... | collective-permute-start | bytes 3342344 | tf_op jit(solution)/shard_map/ppermute | solution.py:137
  43.2 2.4 %collective-permute-done.1.other = bf16[2,4,136,512]{3,2,1,0:T(8,128)(2,1)S(1)} collective-permute-done((bf16[2,4,136,512]{3,2,1,0:T(8,128)(2,1)S(1)}, bf16[2,4,136,512]{3,2,1,0:T(8,128)(2,1)S(1)}, u32[]{:S(2)}, u32[]{:S(2)}) %collective-permute-start.1) | collective-permute-done | bytes 1114144 | tf_op jit(solution)/shard_map/ppermute | solution.py:137
  45.6 0.0 copy-done.3
  45.6 3.3 %shard_map.104 = bf16[512,1024]{1,0:T(8,128)(2,1)S(1)} custom-call(bf16[2,4,136,512]{3,2,1,0:T(8,128)(2,1)S(1)} %bitcast.18, bf16[2,4,136,512]{3,2,1,0:T(8,128)(2,1)S(1)} %collective-permute-done.1.other, bf16[16,2,32,1024]{3,2,1,0:T(8,128)(2,1)S(1)} %bitcast.24), custom_call_target="tpu_custom_call" | custom-call | flops 2147483648 | bytes 6291456 | tf_op jit(solution)/shard_map/pallas_call | solution.py:139
  48.9 0.0 copy-start.4
  48.9 0.0 copy-start.5
  48.9 0.0 copy-start.6
  48.9 23.6 %all_to_all.26 = bf16[4,128,1024]{2,1,0:T(8,128)(2,1)S(1)} all-to-all(bf16[4,128,1024]{2,1,0:T(8,128)(2,1)S(1)} %bitcast.19), channel_id=1, replica_groups=mesh['x'=4,'zf'=2,'zm'=2,'zp'=2,'y'=4,'zh'=2,'c'=2] {'x'}, dimensions={0} | all-to-all | bytes 2097152 | tf_op jit(solution)/shard_map/all_to_all | solution.py:154
  72.6 0.2 add_convert_fusion
  72.7 22.5 %all_to_all.27 = bf16[4,32,1024]{2,1,0:T(8,128)(2,1)S(1)} all-to-all(bf16[4,32,1024]{2,1,0:T(8,128)(2,1)S(1)} %bitcast.26), channel_id=1, replica_groups=mesh['x'=4,'zf'=2,'zm'=2,'zp'=2,'y'=4,'zh'=2,'c'=2] {'zf','zm'}, dimensions={0} | all-to-all | bytes 524288 | tf_op jit(solution)/shard_map/all_to_all | solution.py:156
  95.2 0.0 copy-done.4
  95.2 0.0 copy-done.5
  95.2 0.0 copy-done.6
  95.2 0.8 fusion.2
  96.1 14.3 %all_to_all.28 = bf16[4,32,1024]{2,1,0:T(8,128)(2,1)S(1)} all-to-all(bf16[4,32,1024]{2,1,0:T(8,128)(2,1)S(1)} %broadcast_in_dim.7), channel_id=1, replica_groups=mesh['x'=4,'zf'=2,'zm'=2,'zp'=2,'y'=4,'zh'=2,'c'=2] {'zf','zm'}, dimensions={0} | all-to-all | bytes 524288 | tf_op jit(solution)/shard_map/all_to_all | solution.py:102
  110.4 0.3 broadcast_in_dim.8
  110.6 24.6 %all_to_all.29 = bf16[8,4,32,1024]{3,2,1,0:T(8,128)(2,1)S(1)} all-to-all(bf16[8,4,32,1024]{3,2,1,0:T(8,128)(2,1)S(1)} %broadcast_in_dim.8), channel_id=1, replica_groups=mesh['x'=4,'zf'=2,'zm'=2,'zp'=2,'y'=4,'zh'=2,'c'=2] {'x','zp'}, dimensions={0} | all-to-all | bytes 4194304 | tf_op jit(solution)/shard_map/all_to_all | solution.py:102
  135.3 1.6 %shard_map.105 = bf16[4,4,2,32,1024]{4,3,2,1,0:T(8,128)(2,1)} custom-call(bf16[4,2,4,32,1024]{4,3,2,1,0:T(8,128)(2,1)S(1)} %bitcast.16), custom_call_target="tpu_custom_call" | custom-call | tf_op jit(solution)/shard_map/pallas_call | solution.py:169
  (2 shorter events, 0.0 us)
Async XLA Ops:
  0.6 18.5 %collective-permute-start = (bf16[64,512]{1,0:T(8,128)(2,1)}, bf16[64,512]{1,0:T(8,128)(2,1)S(1)}, u32[]{:S(2)}, u32[]{:S(2)}) collective-permute-start(bf16[64,512]{1,0:T(8,128)(2,1)} %bitcast.20), channel_id=1, source_target_pairs={{0,2},{2,0},{1,3},{3,1},{4,6},{6,4},{5,7},{7,5},{8,10},{10,8},{9,1... | collective-permute-start | bytes 196616 | tf_op jit(solution)/shard_map/ppermute | solution.py:117
  16.9 0.9 copy-start
  17.8 0.7 copy-start.1
  18.5 0.7 copy-start.2
  19.2 26.4 %copy-start.3 = (bf16[1024,1024]{1,0:T(8,128)(2,1)S(1)}, bf16[1024,1024]{1,0:T(8,128)(2,1)}, u32[]{:S(2)}) copy-start(bf16[1024,1024]{1,0:T(8,128)(2,1)} %param.10) | copy-start | bytes 6291460
  37.1 8.5 %collective-permute-start.1 = (bf16[2,4,136,512]{3,2,1,0:T(8,128)(2,1)S(1)}, bf16[2,4,136,512]{3,2,1,0:T(8,128)(2,1)S(1)}, u32[]{:S(2)}, u32[]{:S(2)}) collective-permute-start(bf16[2,4,136,512]{3,2,1,0:T(8,128)(2,1)S(1)} %bitcast.17), channel_id=1, source_target_pairs={{0,1},{1,0},{2,3},{3,2},{4,5},{5,4},{6,7},{7,6},{8,9},{9,8},{10,11... | collective-permute-start | bytes 3342344 | tf_op jit(solution)/shard_map/ppermute | solution.py:137
  48.9 46.3 %copy-start.4 = (f32[32,1024]{1,0:T(8,128)S(1)}, f32[32,1024]{1,0:T(8,128)}, u32[]{:S(2)}) copy-start(f32[32,1024]{1,0:T(8,128)} %param.11) | copy-start | bytes 393220
  48.9 46.3 %copy-start.5 = (f32[32,1024]{1,0:T(8,128)S(1)}, f32[32,1024]{1,0:T(8,128)}, u32[]{:S(2)}) copy-start(f32[32,1024]{1,0:T(8,128)} %param.12) | copy-start | bytes 393220
  48.9 46.3 %copy-start.6 = (f32[32,1024]{1,0:T(8,128)S(1)}, f32[32,1024]{1,0:T(8,128)}, u32[]{:S(2)}) copy-start(f32[32,1024]{1,0:T(8,128)} %param.13) | copy-start | bytes 393220

commit v9 on v8

--- a/solution.py
+++ b/solution.py
@@ -11,7 +11,7 @@
 DP = ("x", "zf", "zm", "zp")
 LABEL = ("y", "zh", "c")
 SWAP = [(0, 1), (1, 0)]
-STAGGER_NS = 10000
+STAGGER_NS = 8000
 
 
 def grad_kernel(own, other, weight, out, whole, rows_w):

time: 137 us -> 137 us (level)
    all_to_all x1, blocking collectives: 23.6 us -> 21.6 us  [per_device(): lax.all_to_all(part.reshape(x_n, zq_n * own_rows, width), 'x', 0, 0, tile...]
    all_to_all x2, blocking collectives: 38.9 us -> 40.6 us  [to_all(): lax.all_to_all(jnp.broadcast_to(array[None], (count, *array.shape)), axes...]
where the time goes in v9:
time: 137 us
  blocking collectives  103 us (75%)
  starting transfers between devices  22.4 us (16%)
  Pallas kernels  4.97 us (4%)
  local copies, waits for them, and re-layouts  2.53 us (2%)
  waiting for transfers between devices  2.36 us (2%)
    all_to_all x2, blocking collectives, to_all(): lax.all_to_all(jnp.broadcast_to(array[None], (count, *array.shape)), axes...  40.6 us
    all_to_all x1, blocking collectives, per_device(): lax.all_to_all(by_x.reshape(zq_n, own_rows, width), ('zf', 'zm'), 0, 0, t...  22.8 us
    all_to_all x1, blocking collectives, per_device(): lax.all_to_all(part.reshape(x_n, zq_n * own_rows, width), 'x', 0, 0, tile...  21.6 us
    all_to_all x1, blocking collectives, per_device(): along_y = lax.all_to_all(sent, ('zp', 'y'), 0, 0, tiled=True)  17.9 us
    ppermute x1, starting transfers between devices, per_device(): far = lax.ppermute(mine, 'zh', SWAP)  16.3 us
    ppermute x1, starting transfers between devices, per_device(): other = lax.ppermute(along_y, 'c', SWAP)  6.09 us
    pallas_call x1, Pallas kernels, per_device(): pl.pallas_call(grad_kernel, out_shape=jax.ShapeDtypeStruct((rows, width),...  3.31 us
  transfers between devices with their start and end apart: 2, of which 1 were waited for; matrix products, arithmetic and copies ran while one was open for 0% of the time, Pallas kernels for 0%

profile of v9, /device:TPU:1, one launch (start us, length us, event | category | flops | bytes accessed | tf_op | source)
XLA Modules:
  0.0 136.8 jit_solution(18352684800735040574)
XLA Ops:
  0.6 16.3 %collective-permute-start = (bf16[64,512]{1,0:T(8,128)(2,1)}, bf16[64,512]{1,0:T(8,128)(2,1)S(1)}, u32[]{:S(2)}, u32[]{:S(2)}) collective-permute-start(bf16[64,512]{1,0:T(8,128)(2,1)} %bitcast.20), channel_id=1, source_target_pairs={{0,2},{2,0},{1,3},{3,1},{4,6},{6,4},{5,7},{7,5},{8,10},{10,8},{9,1... | collective-permute-start | bytes 196616 | tf_op jit(solution)/shard_map/ppermute | solution.py:117
  16.9 0.0 copy-start
  16.9 0.8 copy-done
  17.8 0.0 copy-start.1
  17.8 0.7 copy-done.1
  18.5 0.0 copy-start.2
  18.5 0.7 copy-done.2
  19.2 0.0 copy-start.3
  19.2 0.0 collective-permute-done.far
  19.2 0.1 shard_map.103
  19.3 17.9 %all_to_all.25 = bf16[8,136,512]{2,1,0:T(8,128)(2,1)S(1)} all-to-all(bf16[8,136,512]{2,1,0:T(8,128)(2,1)S(1)} %shard_map.103), channel_id=1, replica_groups=mesh['x'=4,'zf'=2,'zm'=2,'zp'=2,'y'=4,'zh'=2,'c'=2] {'zp','y'}, dimensions={0} | all-to-all | bytes 2228224 | tf_op jit(solution)/shard_map/all_to_all | solution.py:135
  37.1 6.1 %collective-permute-start.1 = (bf16[2,4,136,512]{3,2,1,0:T(8,128)(2,1)S(1)}, bf16[2,4,136,512]{3,2,1,0:T(8,128)(2,1)S(1)}, u32[]{:S(2)}, u32[]{:S(2)}) collective-permute-start(bf16[2,4,136,512]{3,2,1,0:T(8,128)(2,1)S(1)} %bitcast.17), channel_id=1, source_target_pairs={{0,1},{1,0},{2,3},{3,2},{4,5},{5,4},{6,7},{7,6},{8,9},{9,8},{10,11... | collective-permute-start | bytes 3342344 | tf_op jit(solution)/shard_map/ppermute | solution.py:137
  43.2 2.4 %collective-permute-done.1.other = bf16[2,4,136,512]{3,2,1,0:T(8,128)(2,1)S(1)} collective-permute-done((bf16[2,4,136,512]{3,2,1,0:T(8,128)(2,1)S(1)}, bf16[2,4,136,512]{3,2,1,0:T(8,128)(2,1)S(1)}, u32[]{:S(2)}, u32[]{:S(2)}) %collective-permute-start.1) | collective-permute-done | bytes 1114144 | tf_op jit(solution)/shard_map/ppermute | solution.py:137
  45.6 0.0 copy-done.3
  45.6 3.3 %shard_map.104 = bf16[512,1024]{1,0:T(8,128)(2,1)S(1)} custom-call(bf16[2,4,136,512]{3,2,1,0:T(8,128)(2,1)S(1)} %bitcast.18, bf16[2,4,136,512]{3,2,1,0:T(8,128)(2,1)S(1)} %collective-permute-done.1.other, bf16[16,2,32,1024]{3,2,1,0:T(8,128)(2,1)S(1)} %bitcast.24), custom_call_target="tpu_custom_call" | custom-call | flops 2147483648 | bytes 6291456 | tf_op jit(solution)/shard_map/pallas_call | solution.py:139
  48.9 0.0 copy-start.4
  48.9 0.0 copy-start.5
  48.9 0.0 copy-start.6
  48.9 21.6 %all_to_all.26 = bf16[4,128,1024]{2,1,0:T(8,128)(2,1)S(1)} all-to-all(bf16[4,128,1024]{2,1,0:T(8,128)(2,1)S(1)} %bitcast.19), channel_id=1, replica_groups=mesh['x'=4,'zf'=2,'zm'=2,'zp'=2,'y'=4,'zh'=2,'c'=2] {'x'}, dimensions={0} | all-to-all | bytes 2097152 | tf_op jit(solution)/shard_map/all_to_all | solution.py:154
  70.6 0.2 add_convert_fusion
  70.7 22.8 %all_to_all.27 = bf16[4,32,1024]{2,1,0:T(8,128)(2,1)S(1)} all-to-all(bf16[4,32,1024]{2,1,0:T(8,128)(2,1)S(1)} %bitcast.26), channel_id=1, replica_groups=mesh['x'=4,'zf'=2,'zm'=2,'zp'=2,'y'=4,'zh'=2,'c'=2] {'zf','zm'}, dimensions={0} | all-to-all | bytes 524288 | tf_op jit(solution)/shard_map/all_to_all | solution.py:156
  93.5 0.0 copy-done.4
  93.5 0.0 copy-done.5
  93.5 0.0 copy-done.6
  93.5 0.8 fusion.2
  94.4 15.7 %all_to_all.28 = bf16[4,32,1024]{2,1,0:T(8,128)(2,1)S(1)} all-to-all(bf16[4,32,1024]{2,1,0:T(8,128)(2,1)S(1)} %broadcast_in_dim.7), channel_id=1, replica_groups=mesh['x'=4,'zf'=2,'zm'=2,'zp'=2,'y'=4,'zh'=2,'c'=2] {'zf','zm'}, dimensions={0} | all-to-all | bytes 524288 | tf_op jit(solution)/shard_map/all_to_all | solution.py:102
  110.1 0.3 broadcast_in_dim.8
  110.4 24.8 %all_to_all.29 = bf16[8,4,32,1024]{3,2,1,0:T(8,128)(2,1)S(1)} all-to-all(bf16[8,4,32,1024]{3,2,1,0:T(8,128)(2,1)S(1)} %broadcast_in_dim.8), channel_id=1, replica_groups=mesh['x'=4,'zf'=2,'zm'=2,'zp'=2,'y'=4,'zh'=2,'c'=2] {'x','zp'}, dimensions={0} | all-to-all | bytes 4194304 | tf_op jit(solution)/shard_map/all_to_all | solution.py:102
  135.2 1.6 %shard_map.105 = bf16[4,4,2,32,1024]{4,3,2,1,0:T(8,128)(2,1)} custom-call(bf16[4,2,4,32,1024]{4,3,2,1,0:T(8,128)(2,1)S(1)} %bitcast.16), custom_call_target="tpu_custom_call" | custom-call | tf_op jit(solution)/shard_map/pallas_call | solution.py:169
  (2 shorter events, 0.0 us)
Async XLA Ops:
  0.6 18.5 %collective-permute-start = (bf16[64,512]{1,0:T(8,128)(2,1)}, bf16[64,512]{1,0:T(8,128)(2,1)S(1)}, u32[]{:S(2)}, u32[]{:S(2)}) collective-permute-start(bf16[64,512]{1,0:T(8,128)(2,1)} %bitcast.20), channel_id=1, source_target_pairs={{0,2},{2,0},{1,3},{3,1},{4,6},{6,4},{5,7},{7,5},{8,10},{10,8},{9,1... | collective-permute-start | bytes 196616 | tf_op jit(solution)/shard_map/ppermute | solution.py:117
  16.9 0.9 copy-start
  17.8 0.7 copy-start.1
  18.5 0.7 copy-start.2
  19.2 26.4 %copy-start.3 = (bf16[1024,1024]{1,0:T(8,128)(2,1)S(1)}, bf16[1024,1024]{1,0:T(8,128)(2,1)}, u32[]{:S(2)}) copy-start(bf16[1024,1024]{1,0:T(8,128)(2,1)} %param.10) | copy-start | bytes 6291460
  37.1 8.5 %collective-permute-start.1 = (bf16[2,4,136,512]{3,2,1,0:T(8,128)(2,1)S(1)}, bf16[2,4,136,512]{3,2,1,0:T(8,128)(2,1)S(1)}, u32[]{:S(2)}, u32[]{:S(2)}) collective-permute-start(bf16[2,4,136,512]{3,2,1,0:T(8,128)(2,1)S(1)} %bitcast.17), channel_id=1, source_target_pairs={{0,1},{1,0},{2,3},{3,2},{4,5},{5,4},{6,7},{7,6},{8,9},{9,8},{10,11... | collective-permute-start | bytes 3342344 | tf_op jit(solution)/shard_map/ppermute | solution.py:137
  48.9 44.6 %copy-start.4 = (f32[32,1024]{1,0:T(8,128)S(1)}, f32[32,1024]{1,0:T(8,128)}, u32[]{:S(2)}) copy-start(f32[32,1024]{1,0:T(8,128)} %param.11) | copy-start | bytes 393220
  48.9 44.6 %copy-start.5 = (f32[32,1024]{1,0:T(8,128)S(1)}, f32[32,1024]{1,0:T(8,128)}, u32[]{:S(2)}) copy-start(f32[32,1024]{1,0:T(8,128)} %param.12) | copy-start | bytes 393220
  48.9 44.6 %copy-start.6 = (f32[32,1024]{1,0:T(8,128)S(1)}, f32[32,1024]{1,0:T(8,128)}, u32[]{:S(2)}) copy-start(f32[32,1024]{1,0:T(8,128)} %param.13) | copy-start | bytes 393220
